TPU v7x, 512 devices: a whole 4x4x16 slice. The times are simulated.
512 devices in a mesh: tm: 16 (over z_lo, core), tmpl: 32 (over z_hi, y, x).
Axes of the slice: x: 4, y: 4, z: 16 (z_hi: 2, z_lo: 8; z = z_hi * 8 + z_lo), core: 2. Of those that a mesh axis runs over, the one named last changes fastest.
Arguments:
- waveforms: bfloat16 [3072, 3, 12288], P('tmpl', None, 'tm'), may hold values from -360 to 360
- templates: bfloat16 [32, 16, 48, 600], P('tmpl', 'tm'), may hold values from -6 to 6
- group_stations: int32 [32, 16], replicated, may hold values from 0 to 3071, as said below
- template_rows: int32 [32, 16, 16], P('tmpl'), may hold values from 0 to 15, as said below
- moveouts: int32 [32, 16, 16], P('tmpl'), may hold values from 0 to 127, as said below
Outputs:
- network_stack: float32 [32, 16, 12288], P('tmpl', None, 'tm')
Inputs may be any that keep to these rules, and one draw needn't show every extreme that they name: `group_stations`: A group's stations are distinct; at most 2 of them have the same station id // 96, and in every group some value of station id // 96 is shared by exactly 2 of them. `template_rows`: A template's 16 entries are distinct, and every position of a group's table is named by exactly 16 of the group's templates. `moveouts`: in every template some station has moveout 0 and another has 127.
All inputs are finite; a program needn't handle non-finite values.
Results may differ from a plain program's by a relative error of at most 0.0059.
Values may be sent and summed in bfloat16 or wider, within the bound.
A program may use at most 64 MiB of HBM per device.

v0:
```python
import jax
import jax.numpy as jnp
from jax import lax
from jax.sharding import PartitionSpec as P

OFFMAX = 128


def shifted(value, axis, steps):
    count = lax.axis_size(axis)
    initial, last = (max(0, -steps), min(count, count - steps))
    return lax.ppermute(value, axis, [(source, source + steps) for source in range(initial, last)])


def normalize(raw):
    values = raw.astype(jnp.float32)
    centred = values - jnp.mean(values, axis=-1, keepdims=True)
    factor = lax.rsqrt(jnp.sum(centred * centred, axis=-1, keepdims=True) + 1e-06)
    return (centred * factor).astype(jnp.bfloat16)


def fetch_rows(source, group_stations, capacity, station_count, own_index):
    groups, table_size = group_stations.shape
    owners = group_stations // station_count
    row_local = group_stations % station_count
    position = jnp.arange(table_size, dtype=jnp.int32)
    same_owner = owners[:, :, None] == owners[:, None, :]
    earlier = position[:, None] > position[None, :]
    owner_rank = jnp.sum((same_owner & earlier[None]).astype(jnp.int32), axis=2)
    slot_ids = jnp.arange(capacity, dtype=jnp.int32)
    matched = (owners[:, :, None] == own_index) & (
        owner_rank[:, :, None] == slot_ids[None, None, :]
    )
    picked = jnp.sum(jnp.where(matched, row_local[:, :, None], 0), axis=1)
    filled = jnp.any(matched, axis=1)
    outgoing = jnp.take(source, picked.reshape(-1), axis=0)
    outgoing = jnp.where(filled.reshape(-1)[:, None, None], outgoing, jnp.zeros_like(outgoing))
    outgoing = outgoing.reshape(groups, capacity, source.shape[1], source.shape[2])
    incoming = lax.all_to_all(outgoing, "tmpl", split_axis=0, concat_axis=0, tiled=True)
    arrived = incoming.reshape(groups * capacity, source.shape[1], source.shape[2])
    mine_owner = jnp.take(owners, own_index, axis=0)
    mine_rank = jnp.take(owner_rank, own_index, axis=0)
    return jnp.take(arrived, mine_owner * capacity + mine_rank, axis=0)


def channel_ratios(trace, weights, samples, max_shift, tap_count):
    length = trace.shape[0]
    blocks = length // 128
    pieces = trace.reshape(blocks, 128)
    paired = jnp.concatenate([pieces[:-1], pieces[1:]], axis=1)
    hankel = jnp.stack([paired[:, column : column + 128] for column in range(128)], axis=1)
    products = jnp.einsum("aqr,qm->mar", hankel, weights, preferred_element_type=jnp.float32)
    tap_blocks = (tap_count + 127) // 128
    use_count = weights.shape[1] // tap_blocks
    starts = (samples + max_shift) // 128
    products = products.reshape(tap_blocks, use_count, blocks - 1, 128)
    numerator = sum(
        (
            products[block_index, :, block_index : block_index + starts]
            for block_index in range(tap_blocks)
        )
    )
    span_width = starts * 128
    numerator = numerator.reshape(use_count, span_width)
    values = trace.astype(jnp.float32)
    zeros_col = jnp.zeros((1,), jnp.float32)
    running = jnp.concatenate([zeros_col, jnp.cumsum(values)])
    running_sq = jnp.concatenate([zeros_col, jnp.cumsum(values * values)])
    window_sum = running[tap_count : tap_count + span_width] - running[:span_width]
    window_sq = running_sq[tap_count : tap_count + span_width] - running_sq[:span_width]
    spread = jnp.sqrt(jnp.maximum(window_sq - window_sum * window_sum / tap_count, 1.0))
    return numerator / spread[None, :]


def correlate_row(record, weights, offsets, samples, max_shift, tap_count):
    ratios = channel_ratios(record[0], weights[0], samples, max_shift, tap_count)
    for channel in range(1, record.shape[0]):
        ratios = ratios + channel_ratios(
            record[channel], weights[channel], samples, max_shift, tap_count
        )
    return jax.vmap(lambda series, offset: lax.dynamic_slice_in_dim(series, offset, samples))(
        ratios, offsets
    )


def per_device(waveforms, templates, group_stations, template_rows, moveouts):
    groups = lax.axis_size("tmpl")
    own_index = lax.axis_index("tmpl")
    station_count = waveforms.shape[0]
    samples = waveforms.shape[2]
    table_size = group_stations.shape[1]
    capacity = max(2, 2 * table_size // groups)
    tap_count = templates.shape[3]
    padded_taps = (tap_count + 127) // 128 * 128
    extent = OFFMAX + padded_taps
    heading = shifted(waveforms, "tm", -1)
    extended = jnp.concatenate([waveforms, heading], axis=2)
    station_rows = fetch_rows(extended, group_stations, capacity, station_count, own_index)
    shaped = normalize(lax.all_gather(templates, "tm", axis=1, tiled=True))
    station_lists = template_rows[0]
    station_delays = moveouts[0]
    tpl_count, per_template = station_lists.shape
    shaped = shaped[0].reshape(tpl_count, per_template, 3, tap_count)
    shaped = jnp.pad(shaped, ((0, 0), (0, 0), (0, 0), (0, padded_taps - tap_count)))
    matches_row = (
        station_lists[:, :, None] == jnp.arange(table_size, dtype=jnp.int32)[None, None, :]
    )
    usage_mask = jnp.any(matches_row, axis=1).astype(jnp.int32)
    station_slot = jnp.sum(
        jnp.where(matches_row, jnp.arange(per_template, dtype=jnp.int32)[None, :, None], 0), axis=1
    )
    station_shift = jnp.sum(jnp.where(matches_row, station_delays[:, :, None], 0), axis=1)
    order_rank = jnp.cumsum(usage_mask, axis=0) - 1
    use_count = tpl_count * per_template // table_size
    chosen = (usage_mask[:, :, None] == 1) & (
        order_rank[:, :, None] == jnp.arange(use_count, dtype=jnp.int32)[None, None, :]
    )
    template_ids = jnp.arange(tpl_count, dtype=jnp.int32)
    user_ids = jnp.sum(jnp.where(chosen, template_ids[:, None, None], 0), axis=0)
    user_slots = jnp.sum(jnp.where(chosen, station_slot[:, :, None], 0), axis=0)
    user_shifts = jnp.sum(jnp.where(chosen, station_shift[:, :, None], 0), axis=0)
    tap_blocks = padded_taps // 128
    selected = shaped[user_ids, user_slots]
    selected = selected.reshape(table_size, use_count, 3, tap_blocks, 128)
    selected = selected.transpose(0, 2, 4, 3, 1).reshape(table_size, 3, 128, tap_blocks * use_count)

    def one_turn(inputs):
        record, weights, shifts = inputs
        return correlate_row(record, weights, shifts, samples, OFFMAX, tap_count)

    partial_rows = lax.map(one_turn, (station_rows, selected, user_shifts))
    placing = chosen.transpose(1, 2, 0).astype(jnp.float32)
    stacked = jnp.einsum("jun,jut->tn", partial_rows, placing, precision=lax.Precision.HIGHEST)
    return stacked[None]


def solution(mesh):
    in_specs = (
        P("tmpl", None, "tm"),
        P("tmpl", "tm", None, None),
        P(),
        P("tmpl", None, None),
        P("tmpl", None, None),
    )
    out_specs = P("tmpl", None, "tm")
    return jax.shard_map(
        per_device, mesh=mesh, in_specs=in_specs, out_specs=out_specs, check_vma=False
    )
```

profile of v0, /device:TPU:1, one launch (start us, length us, event | category | flops | bytes accessed | tf_op | source)
XLA Modules:
  0.0 930.7 jit_solution(6990916128824988101)
XLA Ops:
  0.0 8.8 collective-permute-start
  8.8 1.4 copy.13366
  17.2 17.8 %all-to-all-start = ((bf16[32,2,3,1536]{3,1,2,0:T(2,128)(2,1)}), bf16[32,2,3,1536]{3,1,2,0:T(2,128)(2,1)S(1)}, u32[]{:S(2)}, u32[]{:S(2)}) async-start(bf16[32,2,3,1536]{3,1,2,0:T(2,128)(2,1)} %copy.13369), calls=%async_computation | async-start | bytes 1179648 | tf_op jit(solution)/shard_map/all_to_all | solution.py:39
  35.5 54.4 %all_gather.3 = bf16[1,16,48,600]{3,2,0,1:T(8,128)(2,1)S(1)} all-gather(bf16[1,1,48,600]{3,2,0,1:T(8,128)(2,1)S(1)} %bitcast.1157), channel_id=1, replica_groups=mesh['tm'=16,'tmpl'=32] {'tm'}, dimensions={1}, use_global_device_ids=true | all-gather | bytes 979200 | tf_op jit(solution)/shard_map/all_gather | solution.py:99
  91.6 2.3 gather_fusion
  97.0 832.4 %while.14 = (s32[]{:T(128)}, f32[16,16,768]{2,1,0:T(8,128)S(1)}, bf16[16,3,128,80]{2,3,1,0:T(8,128)(2,1)S(1)}, bf16[16,3,1536]{2,1,0:T(4,128)(2,1)S(1)}, s32[16,...) while((s32[]{:T(128)}, f32[16,16,768]{2,1,0:T(8,128)S(1)}, ...), condition=%wide.region_25.27_spmd, body=%wide.region_12.26_spmd.sunk | while | flops 90108336 | bytes 10320754 | solution.py:131
  100.7 1.3 stack.1166
  105.6 1.3 stack.1165
  110.5 1.3 stack.1164
  115.9 33.3 %while.15 = (s32[]{:T(128)}, f32[16,896]{1,0:T(8,128)S(1)}, s32[16,2]{0,1:T(2,128)S(1)}, f32[16,768]{1,0:T(8,128)S(1)}, s32[]{:T(128)}, /*index=5*/s32[]{:T(128)}) while((s32[]{:T(128)}, f32[16,896]{1,0:T(8,128)S(1)}, s32[16,2]{0,1:T(2,128)S(1)}, f32[16,768]{1,0:T(8,128)S(1)}, s32[]{:T(128)}, /*index=5*/s32[]{:T(128)}) %tuple.500), condition=%wide.while_cond.1, body=%wide.while_body.1.sunk | while | flops 2 | bytes 12401 | solution.py:81
  152.7 1.3 stack.1166
  157.6 1.3 stack.1165
  162.5 1.3 stack.1164
  167.9 33.3 %while.15 = (s32[]{:T(128)}, f32[16,896]{1,0:T(8,128)S(1)}, s32[16,2]{0,1:T(2,128)S(1)}, f32[16,768]{1,0:T(8,128)S(1)}, s32[]{:T(128)}, /*index=5*/s32[]{:T(128)}) while((s32[]{:T(128)}, f32[16,896]{1,0:T(8,128)S(1)}, s32[16,2]{0,1:T(2,128)S(1)}, f32[16,768]{1,0:T(8,128)S(1)}, s32[]{:T(128)}, /*index=5*/s32[]{:T(128)}) %tuple.500), condition=%wide.while_cond.1, body=%wide.while_body.1.sunk | while | flops 2 | bytes 12401 | solution.py:81
  204.7 1.3 stack.1166
  209.6 1.3 stack.1165
  214.5 1.3 stack.1164
  220.0 33.3 %while.15 = (s32[]{:T(128)}, f32[16,896]{1,0:T(8,128)S(1)}, s32[16,2]{0,1:T(2,128)S(1)}, f32[16,768]{1,0:T(8,128)S(1)}, s32[]{:T(128)}, /*index=5*/s32[]{:T(128)}) while((s32[]{:T(128)}, f32[16,896]{1,0:T(8,128)S(1)}, s32[16,2]{0,1:T(2,128)S(1)}, f32[16,768]{1,0:T(8,128)S(1)}, s32[]{:T(128)}, /*index=5*/s32[]{:T(128)}) %tuple.500), condition=%wide.while_cond.1, body=%wide.while_body.1.sunk | while | flops 2 | bytes 12401 | solution.py:81
  256.7 1.3 stack.1166
  261.7 1.3 stack.1165
  266.5 1.3 stack.1164
  272.0 33.3 %while.15 = (s32[]{:T(128)}, f32[16,896]{1,0:T(8,128)S(1)}, s32[16,2]{0,1:T(2,128)S(1)}, f32[16,768]{1,0:T(8,128)S(1)}, s32[]{:T(128)}, /*index=5*/s32[]{:T(128)}) while((s32[]{:T(128)}, f32[16,896]{1,0:T(8,128)S(1)}, s32[16,2]{0,1:T(2,128)S(1)}, f32[16,768]{1,0:T(8,128)S(1)}, s32[]{:T(128)}, /*index=5*/s32[]{:T(128)}) %tuple.500), condition=%wide.while_cond.1, body=%wide.while_body.1.sunk | while | flops 2 | bytes 12401 | solution.py:81
  308.8 1.3 stack.1166
  313.7 1.3 stack.1165
  318.6 1.3 stack.1164
  324.0 33.3 %while.15 = (s32[]{:T(128)}, f32[16,896]{1,0:T(8,128)S(1)}, s32[16,2]{0,1:T(2,128)S(1)}, f32[16,768]{1,0:T(8,128)S(1)}, s32[]{:T(128)}, /*index=5*/s32[]{:T(128)}) while((s32[]{:T(128)}, f32[16,896]{1,0:T(8,128)S(1)}, s32[16,2]{0,1:T(2,128)S(1)}, f32[16,768]{1,0:T(8,128)S(1)}, s32[]{:T(128)}, /*index=5*/s32[]{:T(128)}) %tuple.500), condition=%wide.while_cond.1, body=%wide.while_body.1.sunk | while | flops 2 | bytes 12401 | solution.py:81
  360.8 1.3 stack.1166
  365.7 1.3 stack.1165
  370.6 1.3 stack.1164
  376.0 33.3 %while.15 = (s32[]{:T(128)}, f32[16,896]{1,0:T(8,128)S(1)}, s32[16,2]{0,1:T(2,128)S(1)}, f32[16,768]{1,0:T(8,128)S(1)}, s32[]{:T(128)}, /*index=5*/s32[]{:T(128)}) while((s32[]{:T(128)}, f32[16,896]{1,0:T(8,128)S(1)}, s32[16,2]{0,1:T(2,128)S(1)}, f32[16,768]{1,0:T(8,128)S(1)}, s32[]{:T(128)}, /*index=5*/s32[]{:T(128)}) %tuple.500), condition=%wide.while_cond.1, body=%wide.while_body.1.sunk | while | flops 2 | bytes 12401 | solution.py:81
  412.8 1.3 stack.1166
  417.7 1.3 stack.1165
  422.6 1.3 stack.1164
  428.0 33.3 %while.15 = (s32[]{:T(128)}, f32[16,896]{1,0:T(8,128)S(1)}, s32[16,2]{0,1:T(2,128)S(1)}, f32[16,768]{1,0:T(8,128)S(1)}, s32[]{:T(128)}, /*index=5*/s32[]{:T(128)}) while((s32[]{:T(128)}, f32[16,896]{1,0:T(8,128)S(1)}, s32[16,2]{0,1:T(2,128)S(1)}, f32[16,768]{1,0:T(8,128)S(1)}, s32[]{:T(128)}, /*index=5*/s32[]{:T(128)}) %tuple.500), condition=%wide.while_cond.1, body=%wide.while_body.1.sunk | while | flops 2 | bytes 12401 | solution.py:81
  464.8 1.3 stack.1166
  469.7 1.3 stack.1165
  474.6 1.3 stack.1164
  480.0 33.3 %while.15 = (s32[]{:T(128)}, f32[16,896]{1,0:T(8,128)S(1)}, s32[16,2]{0,1:T(2,128)S(1)}, f32[16,768]{1,0:T(8,128)S(1)}, s32[]{:T(128)}, /*index=5*/s32[]{:T(128)}) while((s32[]{:T(128)}, f32[16,896]{1,0:T(8,128)S(1)}, s32[16,2]{0,1:T(2,128)S(1)}, f32[16,768]{1,0:T(8,128)S(1)}, s32[]{:T(128)}, /*index=5*/s32[]{:T(128)}) %tuple.500), condition=%wide.while_cond.1, body=%wide.while_body.1.sunk | while | flops 2 | bytes 12401 | solution.py:81
  516.8 1.3 stack.1166
  521.7 1.3 stack.1165
  526.6 1.3 stack.1164
  532.1 33.3 %while.15 = (s32[]{:T(128)}, f32[16,896]{1,0:T(8,128)S(1)}, s32[16,2]{0,1:T(2,128)S(1)}, f32[16,768]{1,0:T(8,128)S(1)}, s32[]{:T(128)}, /*index=5*/s32[]{:T(128)}) while((s32[]{:T(128)}, f32[16,896]{1,0:T(8,128)S(1)}, s32[16,2]{0,1:T(2,128)S(1)}, f32[16,768]{1,0:T(8,128)S(1)}, s32[]{:T(128)}, /*index=5*/s32[]{:T(128)}) %tuple.500), condition=%wide.while_cond.1, body=%wide.while_body.1.sunk | while | flops 2 | bytes 12401 | solution.py:81
  568.8 1.3 stack.1166
  573.8 1.3 stack.1165
  578.6 1.3 stack.1164
  584.1 33.3 %while.15 = (s32[]{:T(128)}, f32[16,896]{1,0:T(8,128)S(1)}, s32[16,2]{0,1:T(2,128)S(1)}, f32[16,768]{1,0:T(8,128)S(1)}, s32[]{:T(128)}, /*index=5*/s32[]{:T(128)}) while((s32[]{:T(128)}, f32[16,896]{1,0:T(8,128)S(1)}, s32[16,2]{0,1:T(2,128)S(1)}, f32[16,768]{1,0:T(8,128)S(1)}, s32[]{:T(128)}, /*index=5*/s32[]{:T(128)}) %tuple.500), condition=%wide.while_cond.1, body=%wide.while_body.1.sunk | while | flops 2 | bytes 12401 | solution.py:81
  620.9 1.3 stack.1166
  625.8 1.3 stack.1165
  630.7 1.3 stack.1164
  636.1 33.3 %while.15 = (s32[]{:T(128)}, f32[16,896]{1,0:T(8,128)S(1)}, s32[16,2]{0,1:T(2,128)S(1)}, f32[16,768]{1,0:T(8,128)S(1)}, s32[]{:T(128)}, /*index=5*/s32[]{:T(128)}) while((s32[]{:T(128)}, f32[16,896]{1,0:T(8,128)S(1)}, s32[16,2]{0,1:T(2,128)S(1)}, f32[16,768]{1,0:T(8,128)S(1)}, s32[]{:T(128)}, /*index=5*/s32[]{:T(128)}) %tuple.500), condition=%wide.while_cond.1, body=%wide.while_body.1.sunk | while | flops 2 | bytes 12401 | solution.py:81
  672.9 1.3 stack.1166
  677.8 1.3 stack.1165
  682.7 1.3 stack.1164
  688.1 33.3 %while.15 = (s32[]{:T(128)}, f32[16,896]{1,0:T(8,128)S(1)}, s32[16,2]{0,1:T(2,128)S(1)}, f32[16,768]{1,0:T(8,128)S(1)}, s32[]{:T(128)}, /*index=5*/s32[]{:T(128)}) while((s32[]{:T(128)}, f32[16,896]{1,0:T(8,128)S(1)}, s32[16,2]{0,1:T(2,128)S(1)}, f32[16,768]{1,0:T(8,128)S(1)}, s32[]{:T(128)}, /*index=5*/s32[]{:T(128)}) %tuple.500), condition=%wide.while_cond.1, body=%wide.while_body.1.sunk | while | flops 2 | bytes 12401 | solution.py:81
  724.9 1.3 stack.1166
  734.7 1.3 stack.1164
  740.1 33.3 %while.15 = (s32[]{:T(128)}, f32[16,896]{1,0:T(8,128)S(1)}, s32[16,2]{0,1:T(2,128)S(1)}, f32[16,768]{1,0:T(8,128)S(1)}, s32[]{:T(128)}, /*index=5*/s32[]{:T(128)}) while((s32[]{:T(128)}, f32[16,896]{1,0:T(8,128)S(1)}, s32[16,2]{0,1:T(2,128)S(1)}, f32[16,768]{1,0:T(8,128)S(1)}, s32[]{:T(128)}, /*index=5*/s32[]{:T(128)}) %tuple.500), condition=%wide.while_cond.1, body=%wide.while_body.1.sunk | while | flops 2 | bytes 12401 | solution.py:81
  776.9 1.3 stack.1166
  792.1 33.3 %while.15 = (s32[]{:T(128)}, f32[16,896]{1,0:T(8,128)S(1)}, s32[16,2]{0,1:T(2,128)S(1)}, f32[16,768]{1,0:T(8,128)S(1)}, s32[]{:T(128)}, /*index=5*/s32[]{:T(128)}) while((s32[]{:T(128)}, f32[16,896]{1,0:T(8,128)S(1)}, s32[16,2]{0,1:T(2,128)S(1)}, f32[16,768]{1,0:T(8,128)S(1)}, s32[]{:T(128)}, /*index=5*/s32[]{:T(128)}) %tuple.500), condition=%wide.while_cond.1, body=%wide.while_body.1.sunk | while | flops 2 | bytes 12401 | solution.py:81
  828.9 1.3 stack.1166
  833.8 1.3 stack.1165
  844.2 33.3 %while.15 = (s32[]{:T(128)}, f32[16,896]{1,0:T(8,128)S(1)}, s32[16,2]{0,1:T(2,128)S(1)}, f32[16,768]{1,0:T(8,128)S(1)}, s32[]{:T(128)}, /*index=5*/s32[]{:T(128)}) while((s32[]{:T(128)}, f32[16,896]{1,0:T(8,128)S(1)}, s32[16,2]{0,1:T(2,128)S(1)}, f32[16,768]{1,0:T(8,128)S(1)}, s32[]{:T(128)}, /*index=5*/s32[]{:T(128)}) %tuple.500), condition=%wide.while_cond.1, body=%wide.while_body.1.sunk | while | flops 2 | bytes 12401 | solution.py:81
  885.9 1.3 stack.1165
  896.2 33.3 %while.15 = (s32[]{:T(128)}, f32[16,896]{1,0:T(8,128)S(1)}, s32[16,2]{0,1:T(2,128)S(1)}, f32[16,768]{1,0:T(8,128)S(1)}, s32[]{:T(128)}, /*index=5*/s32[]{:T(128)}) while((s32[]{:T(128)}, f32[16,896]{1,0:T(8,128)S(1)}, s32[16,2]{0,1:T(2,128)S(1)}, f32[16,768]{1,0:T(8,128)S(1)}, s32[]{:T(128)}, /*index=5*/s32[]{:T(128)}) %tuple.500), condition=%wide.while_cond.1, body=%wide.while_body.1.sunk | while | flops 2 | bytes 12401 | solution.py:81
  (8734 shorter events, 727.4 us)
Async XLA Ops:
  0.0 13.1 %collective-permute-start = (bf16[96,3,768]{2,0,1:T(8,128)(2,1)}, bf16[96,3,768]{2,0,1:T(8,128)(2,1)S(1)}, u32[]{:S(2)}, u32[]{:S(2)}) collective-permute-start(bf16[96,3,768]{2,0,1:T(8,128)(2,1)} %param.9), channel_id=1, source_target_pairs={{32,0},{64,32},{96,64},{128,96},{160,128},{192,160},{224,192},{256... | collective-permute-start | bytes 1327112 | tf_op jit(solution)/shard_map/ppermute | solution.py:12
  15.8 19.2 %copy-start.2 = (s32[1,16,16]{2,1,0:T(8,128)S(1)}, s32[1,16,16]{2,1,0:T(8,128)}, u32[]{:S(2)}) copy-start(s32[1,16,16]{2,1,0:T(8,128)} %param.12) | copy-start | bytes 3076
  15.8 19.2 %copy-start.3 = (s32[1,16,16]{2,1,0:T(8,128)S(1)}, s32[1,16,16]{2,1,0:T(8,128)}, u32[]{:S(2)}) copy-start(s32[1,16,16]{2,1,0:T(8,128)} %param.13) | copy-start | bytes 3076
  15.8 19.6 %copy-start.1 = (bf16[1,1,48,600]{3,2,1,0:T(8,128)(2,1)S(1)}, bf16[1,1,48,600]{3,2,1,0:T(8,128)(2,1)}, u32[]{:S(2)}) copy-start(bf16[1,1,48,600]{3,2,1,0:T(8,128)(2,1)} %param.10) | copy-start | bytes 172804
  17.2 78.7 %all-to-all-start = ((bf16[32,2,3,1536]{3,1,2,0:T(2,128)(2,1)}), bf16[32,2,3,1536]{3,1,2,0:T(2,128)(2,1)S(1)}, u32[]{:S(2)}, u32[]{:S(2)}) async-start(bf16[32,2,3,1536]{3,1,2,0:T(2,128)(2,1)} %copy.13369), calls=%async_computation | async-start | bytes 1179648 | tf_op jit(solution)/shard_map/all_to_all | solution.py:39
  95.5 1.6 copy-start
where the time goes:
time: 936 us; the launch traced here: 931 us
  local copies, waits for them, and re-layouts  662 us (71%)
  other arithmetic  113 us (12%)
  loops' own time  62.4 us (7%)
  blocking collectives  54.4 us (6%)
  starting transfers between devices  26.6 us (3%)
  matrix products  11.3 us (1%)
    gather x1024, local copies, waits for them, and re-layouts  527 us
    another operation x6160, local copies, waits for them, and re-layouts, channel_ratios(): jnp.stack([paired[:, column:column + 128] for column in range(128)], axis=1)  105 us
    another operation x720, other arithmetic, channel_ratios(): jnp.stack([paired[:, column:column + 128] for column in range(128)], axis=1)  65.6 us
    another operation x1, loops' own time, per_device(): partial_rows = lax.map(one_turn, (station_rows, selected, user_shifts))  56.2 us
    all_gather x1, blocking collectives, per_device(): shaped = normalize(lax.all_gather(templates, 'tm', axis=1, tiled=True))  54.4 us
    another operation x272, other arithmetic  36.3 us

commit v1 on v0

v1 whole, which is shorter than its diff:
```python
import functools

import jax
import jax.numpy as jnp
from jax import lax
from jax.experimental import pallas as pl
from jax.experimental.pallas import tpu as pltpu
from jax.sharding import PartitionSpec as P

STRIDE = 8
LANES = 128


def iota(shape, dim):
    return lax.broadcasted_iota(jnp.int32, shape, dim)


def correlate_kernel(taps, rowidx, delays, rec_ref, tpl_ref, out_ref, tplf, xa, xb, inv, zs, ws, acc):
    stations = rowidx.shape[0]
    tpls = rowidx.shape[1]
    channels = xa.shape[0] // stations
    nrc = xa.shape[0]
    samples = rec_ref.shape[1]
    frames = samples // STRIDE
    padded = tpl_ref.shape[1]
    kblocks = padded // LANES
    groups = taps // STRIDE + 1
    lane = iota((STRIDE, LANES), 1)
    sub = iota((STRIDE, LANES), 0)

    tplf[...] = tpl_ref[...].astype(jnp.float32)

    gap = iota((samples, LANES), 0) - STRIDE * iota((samples, LANES), 1)
    flat_lane = iota((nrc, LANES), 1)
    for e in range(STRIDE):
        pick = jnp.where(gap == e, 1.0, 0.0).astype(jnp.bfloat16)
        phase = jnp.dot(rec_ref[...], pick, preferred_element_type=jnp.float32)
        later = pltpu.roll(phase[nrc:], frames, axis=1)
        xa[:, e, :] = jnp.where(flat_lane < frames, phase[:nrc], later)
        xb[:, e, :] = later

    ahead = iota((2 * LANES, LANES), 0) - iota((2 * LANES, LANES), 1)
    band = jnp.where((ahead >= 0) & (ahead < taps // STRIDE), 1.0, 0.0).astype(jnp.bfloat16)
    flat = jnp.concatenate([xa[...].reshape(nrc * STRIDE, LANES), xb[...].reshape(nrc * STRIDE, LANES)], axis=1)
    square = flat * flat
    high = square.astype(jnp.bfloat16)
    low = (square - high.astype(jnp.float32)).astype(jnp.bfloat16)

    def banded(v):
        return jnp.dot(v, band, preferred_element_type=jnp.float32)

    def octet(v):
        v = v.reshape(nrc, STRIDE, LANES)
        row = iota((nrc, STRIDE, LANES), 1)
        for k in (1, 2, 4):
            nxt = pltpu.roll(v, LANES - 1, axis=2)
            v = v + pltpu.roll(jnp.where(row < k, nxt, v), STRIDE - k, axis=1)
        return v

    wsum = octet(banded(flat.astype(jnp.bfloat16)))
    wsq = octet(banded(high) + banded(low))
    inv[...] = lax.rsqrt(jnp.maximum(wsq - wsum * wsum / taps, 1.0))

    acc[...] = jnp.zeros_like(acc)
    for i in range(groups, padded // STRIDE, 2):
        for c in range(channels):
            zs[c, STRIDE * i : STRIDE * (i + 2), :] = jnp.zeros((2 * STRIDE, LANES), jnp.bfloat16)

    def station(r, carry):
        ratio = None
        for c in range(channels):
            rc = r * channels + c
            a, b = xa[rc], xb[rc]
            for i in range(0, groups, 2):
                pair = [
                    pltpu.roll(jnp.where(lane < s, b, a), (LANES - s) % LANES, axis=1) for s in (i, i + 1)
                ]
                zs[c, STRIDE * i : STRIDE * (i + 2), :] = jnp.concatenate(pair, axis=0).astype(jnp.bfloat16)
            for t in range(0, tpls, 2):
                rolled = []
                for tt in (t, t + 1):
                    row = tplf[pl.ds(rowidx[r, tt] + c, 1), :]
                    parts = [
                        pltpu.roll(
                            jnp.broadcast_to(row[:, LANES * k : LANES * (k + 1)], (STRIDE, LANES)),
                            0, axis=1, stride=1, stride_axis=0,
                        )
                        for k in range(kblocks)
                    ]
                    rolled.append(parts)
                for k in range(kblocks):
                    both = [
                        jnp.where(lane < sub, p[k - 1] if k else jnp.zeros_like(p[0]), p[k]) for p in rolled
                    ]
                    ws[c, STRIDE * t : STRIDE * (t + 2), LANES * k : LANES * (k + 1)] = jnp.concatenate(
                        both, axis=0
                    ).astype(jnp.bfloat16)
            numer = jnp.dot(ws[c], zs[c], preferred_element_type=jnp.float32)
            part = numer.reshape(tpls, STRIDE, LANES) * inv[rc][None]
            ratio = part if ratio is None else ratio + part
        for t in range(tpls):
            m = delays[r, t]
            f = m // STRIDE
            e = m - f * STRIDE
            near = pltpu.roll(ratio[t], (LANES - f) % LANES, axis=1)
            far = pltpu.roll(near, LANES - 1, axis=1)
            acc[t] += pltpu.roll(jnp.where(sub < e, far, near), (STRIDE - e) % STRIDE, axis=0)
        return carry

    lax.fori_loop(0, stations, station, 0)

    total = acc[...].reshape(tpls * STRIDE, LANES)
    p1 = total.astype(jnp.bfloat16)
    rest = total - p1.astype(jnp.float32)
    p2 = rest.astype(jnp.bfloat16)
    p3 = (rest - p2.astype(jnp.float32)).astype(jnp.bfloat16)
    spots = iota((LANES, samples), 1) // STRIDE
    spread_out = jnp.where(spots == iota((LANES, samples), 0), 1.0, 0.0).astype(jnp.bfloat16)

    def placed(v):
        return jnp.dot(v, spread_out, preferred_element_type=jnp.float32)

    wide = (placed(p1) + placed(p2) + placed(p3)).reshape(tpls, STRIDE, samples)
    mine = iota((tpls, STRIDE, samples), 2) % STRIDE == iota((tpls, STRIDE, samples), 1)
    out_ref[...] = jnp.sum(jnp.where(mine, wide, 0.0), axis=1)


def correlate(rec, tpl, rowidx, delays, taps):
    stations, tpls = rowidx.shape
    nrc = rec.shape[0] // 2
    samples = rec.shape[1]
    padded = tpl.shape[1]
    channels = nrc // stations
    vm = pl.BlockSpec(memory_space=pltpu.VMEM)
    sm = pl.BlockSpec(memory_space=pltpu.SMEM)
    return pl.pallas_call(
        functools.partial(correlate_kernel, taps),
        out_shape=jax.ShapeDtypeStruct((tpls, samples), jnp.float32),
        in_specs=[sm, sm, vm, vm],
        out_specs=vm,
        scratch_shapes=[
            pltpu.VMEM(tpl.shape, jnp.float32),
            pltpu.VMEM((nrc, STRIDE, LANES), jnp.float32),
            pltpu.VMEM((nrc, STRIDE, LANES), jnp.float32),
            pltpu.VMEM((nrc, STRIDE, LANES), jnp.float32),
            pltpu.VMEM((channels, padded, LANES), jnp.bfloat16),
            pltpu.VMEM((channels, tpls * STRIDE, padded), jnp.bfloat16),
            pltpu.VMEM((tpls, STRIDE, LANES), jnp.float32),
        ],
        compiler_params=pltpu.CompilerParams(vmem_limit_bytes=32 << 20),
    )(rowidx, delays, rec, tpl)


def normalize(raw):
    values = raw.astype(jnp.float32)
    centred = values - jnp.mean(values, axis=-1, keepdims=True)
    factor = lax.rsqrt(jnp.sum(centred * centred, axis=-1, keepdims=True) + 1e-06)
    return (centred * factor).astype(jnp.bfloat16)


def fetch_rows(source, group_stations, capacity, own_index):
    groups, table_size = group_stations.shape
    station_count = source.shape[0]
    owners = group_stations // station_count
    row_local = group_stations % station_count
    position = jnp.arange(table_size, dtype=jnp.int32)
    same_owner = owners[:, :, None] == owners[:, None, :]
    earlier = position[:, None] > position[None, :]
    owner_rank = jnp.sum((same_owner & earlier[None]).astype(jnp.int32), axis=2)
    slot_ids = jnp.arange(capacity, dtype=jnp.int32)
    matched = (owners[:, :, None] == own_index) & (
        owner_rank[:, :, None] == slot_ids[None, None, :]
    )
    picked = jnp.sum(jnp.where(matched, row_local[:, :, None], 0), axis=1)
    outgoing = jnp.take(source, picked.reshape(-1), axis=0)
    outgoing = outgoing.reshape(groups, capacity, source.shape[1], source.shape[2])
    incoming = lax.all_to_all(outgoing, "tmpl", split_axis=0, concat_axis=0, tiled=True)
    arrived = incoming.reshape(groups * capacity, source.shape[1], source.shape[2])
    mine_owner = jnp.take(owners, own_index, axis=0)
    mine_rank = jnp.take(owner_rank, own_index, axis=0)
    return jnp.take(arrived, mine_owner * capacity + mine_rank, axis=0)


def per_device(waveforms, templates, group_stations, template_rows, moveouts):
    groups = lax.axis_size("tmpl")
    windows = lax.axis_size("tm")
    own_index = lax.axis_index("tmpl")
    channels, samples = waveforms.shape[1:]
    table_size = group_stations.shape[1]
    capacity = max(2, 2 * table_size // groups)
    taps = templates.shape[3]
    padded = (taps + LANES - 1) // LANES * LANES
    normed = normalize(templates[0, 0])
    normed = jnp.pad(normed, ((0, 0), (0, padded - taps)))
    tpl = lax.all_gather(normed, "tm", axis=0, tiled=True)
    rows = fetch_rows(waveforms, group_stations, capacity, own_index)
    rows = rows.reshape(table_size * channels, samples)
    later = lax.ppermute(rows, "tm", [(w, w - 1) for w in range(1, windows)])
    rec = jnp.concatenate([rows, later], axis=0)
    lists, shifts = template_rows[0], moveouts[0]
    tpls, per_template = lists.shape
    hit = lists[:, :, None] == jnp.arange(table_size, dtype=jnp.int32)
    slot = jnp.sum(jnp.where(hit, jnp.arange(per_template, dtype=jnp.int32)[None, :, None], 0), axis=1)
    delays = jnp.sum(jnp.where(hit, shifts[:, :, None], 0), axis=1)
    base = jnp.arange(tpls, dtype=jnp.int32)[:, None] * (per_template * channels)
    rowidx = base + slot * channels
    return correlate(rec, tpl, rowidx.T, delays.T, taps)[None]


def solution(mesh):
    in_specs = (
        P("tmpl", None, "tm"),
        P("tmpl", "tm", None, None),
        P(),
        P("tmpl", None, None),
        P("tmpl", None, None),
    )
    out_specs = P("tmpl", None, "tm")
    return jax.shard_map(
        per_device, mesh=mesh, in_specs=in_specs, out_specs=out_specs, check_vma=False
    )
```

time: 936 us -> 89.4 us (0.10)
  local copies, waits for them, and re-layouts: 662 us -> 3.75 us
  other arithmetic: 113 us -> 2.84 us
  loops' own time: 62.4 us -> 0 us
  Pallas kernels: 0 us -> 15.4 us
  blocking collectives: 54.4 us -> 39.9 us
  matrix products: 11.3 us -> 0 us
    gather x1026 -> x0, local copies, waits for them, and re-layouts: 529 us -> none
    another operation x6337 -> x0, local copies, waits for them, and re-layouts: 123 us -> none  [the longest x6160 105 us: channel_ratios(): jnp.stack([paired[:, column:column + 128] for column in range(128)], axis=1)]
    another operation x993 -> x0, other arithmetic: 102 us -> none  [the longest x720 65.6 us: channel_ratios(): jnp.stack([paired[:, column:column + 128] for column in range(128)], axis=1)]
    another operation x17 -> x0, loops' own time: 62.4 us -> none  [the longest x1 56.2 us: per_device(): partial_rows = lax.map(one_turn, (station_rows, selected, user_shifts))]
    pallas_call x0 -> x1, Pallas kernels: none -> 15.4 us  [correlate(): pl.pallas_call(functools.partial(correlate_kernel, taps), out_shape=jax.S...]
    all_gather x1, blocking collectives: 54.4 us -> 39.9 us  [per_device(): tpl = lax.all_gather(normed, 'tm', axis=0, tiled=True)]
    dot_general x49 -> x0, matrix products: 11.3 us -> none  [the longest x48 10.1 us: channel_ratios(): jnp.einsum('aqr,qm->mar', hankel, weights, preferred_element_type=jnp.flo...]
where the time goes in v1:
time: 89.4 us; the launch traced here: 89 us
  blocking collectives  39.9 us (45%)
  starting transfers between devices  23.3 us (26%)
  Pallas kernels  15.4 us (17%)
  local copies, waits for them, and re-layouts  3.75 us (4%)
  waiting for transfers between devices  3.52 us (4%)
  other arithmetic  2.84 us (3%)
    all_gather x1, blocking collectives, per_device(): tpl = lax.all_gather(normed, 'tm', axis=0, tiled=True)  39.9 us
    all_to_all x1, starting transfers between devices, fetch_rows(): lax.all_to_all(outgoing, 'tmpl', split_axis=0, concat_axis=0, tiled=True)  21.3 us
    pallas_call x1, Pallas kernels, correlate(): pl.pallas_call(functools.partial(correlate_kernel, taps), out_shape=jax.S...  15.4 us
    ppermute x1, waiting for transfers between devices, per_device(): later = lax.ppermute(rows, 'tm', [(w, w - 1) for w in range(1, windows)])  3.51 us
    ppermute x1, starting transfers between devices, per_device(): later = lax.ppermute(rows, 'tm', [(w, w - 1) for w in range(1, windows)])  2.06 us
  transfers between devices with their start and end apart: 2, of which 1 were waited for; matrix products, arithmetic and copies ran while one was open for 1% of the time, Pallas kernels for 0%

profile of v1, /device:TPU:1, one launch (start us, length us, event | category | flops | bytes accessed | tf_op | source)
XLA Modules:
  0.0 89.0 jit_solution(3111406772722506046)
XLA Ops:
  0.0 0.0 copy-start
  0.0 0.0 copy-start.2
  0.0 0.8 add_select_fusion
  0.8 0.0 copy-done.2
  0.8 0.1 convert_reduce_fusion.1
  1.0 0.1 copy.30
  1.1 0.1 reshape.88
  1.2 0.0 copy-done
  1.2 1.5 %gather_fusion = bf16[64,3,768]{2,0,1:T(8,128)(2,1)S(1)} fusion(bf16[96,3,768]{2,0,1:T(8,128)(2,1)S(1)} %copy-done, s32[1024]{0:T(1024)S(1)} %pad_clamp_fusion.1), kind=kCustom, calls=%fused_computation | custom fusion | bytes 590080 | tf_op jit(solution)/shard_map/jit(_take)/gather | solution.py:175
  2.7 0.1 gather.16
  2.8 0.1 copy.29
  2.9 1.0 %broadcast_select_fusion = bf16[32,2,3,768]{3,1,2,0:T(2,128)(2,1)} fusion(pred[32,2]{1,0:T(8,128)(4,1)S(1)} %copy.29, bf16[32,2,3,768]{3,1,0,2:T(2,128)(2,1)S(1)} %gather.16), kind=kLoop, calls=%fused_computation.2 | loop fusion | flops 147456 | bytes 589888 | tf_op jit(solution)/shard_map/jit(_take)/select_n | solution.py:175
  4.0 0.0 copy-start.1
  4.0 21.3 %all-to-all-start = ((bf16[32,2,3,768]{3,1,2,0:T(2,128)(2,1)}), bf16[32,2,3,768]{3,1,2,0:T(2,128)(2,1)S(1)}, u32[]{:S(2)}, u32[]{:S(2)}) async-start(bf16[32,2,3,768]{3,1,2,0:T(2,128)(2,1)} %broadcast_select_fusion), calls=%async_computation | async-start | bytes 589824 | tf_op jit(solution)/shard_map/all_to_all | solution.py:177
  25.2 0.2 select_reduce_fusion.3
  25.4 0.0 copy-done.1
  25.4 0.0 copy-start.4
  25.4 0.1 convert_reduce_fusion
  25.5 0.0 copy-start.3
  25.6 0.5 copy-done.4
  26.1 0.1 copy-done.3
  26.3 0.1 select_reduce_fusion
  26.4 0.2 fusion.3
  26.6 0.1 broadcast_in_dim.89
  26.7 0.1 broadcast_in_dim.90
  26.8 0.1 copy.27
  26.8 0.1 fusion.4
  27.0 39.9 %all_gather.3.tpl_ref = bf16[768,640]{1,0:T(8,128)(2,1)S(1)} all-gather(bf16[48,640]{1,0:T(8,128)(2,1)S(1)} %pad.4), channel_id=1, replica_groups=mesh['tm'=16,'tmpl'=32] {'tm'}, dimensions={0}, use_global_device_ids=true | all-gather | bytes 1044480 | tf_op jit(solution)/shard_map/all_gather | solution.py:195
  66.9 0.0 all-to-all-done
  66.9 0.2 copy.32
  67.1 0.6 gather_fusion.1
  67.7 0.1 gather.18
  67.8 0.1 broadcast_select_fusion.1
  67.8 2.1 %collective-permute-start = (bf16[48,768]{1,0:T(8,128)(2,1)S(1)}, bf16[48,768]{1,0:T(8,128)(2,1)S(1)}, u32[]{:S(2)}, u32[]{:S(2)}) collective-permute-start(bf16[48,768]{1,0:T(8,128)(2,1)S(1)} %broadcast_select_fusion.1), channel_id=1, source_target_pairs={{32,0},{64,32},{96,64},{128,96},{160,128},{192,160},{224,192},{256... | collective-permute-start | bytes 221192 | tf_op jit(solution)/shard_map/ppermute | solution.py:198
  69.9 0.1 copy.28
  70.0 3.5 %collective-permute-done = bf16[48,768]{1,0:T(8,128)(2,1)S(1)} collective-permute-done((bf16[48,768]{1,0:T(8,128)(2,1)S(1)}, bf16[48,768]{1,0:T(8,128)(2,1)S(1)}, u32[]{:S(2)}, u32[]{:S(2)}) %collective-permute-start) | collective-permute-done | bytes 73760 | tf_op jit(solution)/shard_map/ppermute | solution.py:198
  73.5 15.4 %shard_map.55 = f32[16,768]{1,0:T(8,128)} custom-call(s32[16,16]{1,0:T(8,128)S(1)} %add_bitcast_fusion.rowidx, s32[16,16]{1,0:T(8,128)S(1)} %bitcast.23, bf16[96,768]{1,0:T(8,128)(2,1)S(1)} %pad_maximum_fusion.rec_ref, bf16[768,640]{1,0:T(8,128)(2,1)S(1)} %all_gather.3.tpl_ref), custom_call_target="tpu_custom_call" | custom-call | tf_op jit(solution)/shard_map/pallas_call | solution.py:136
  (14 shorter events, 0.1 us)
Async XLA Ops:
  0.0 1.2 %copy-start = (bf16[96,3,768]{2,0,1:T(8,128)(2,1)S(1)}, bf16[96,3,768]{2,0,1:T(8,128)(2,1)}, u32[]{:S(2)}) copy-start(bf16[96,3,768]{2,0,1:T(8,128)(2,1)} %param.7) | copy-start | bytes 1327108
  0.0 0.8 copy-start.2
  4.0 21.5 %copy-start.1 = (bf16[1,1,48,600]{3,2,1,0:T(8,128)(2,1)S(1)}, bf16[1,1,48,600]{3,2,1,0:T(8,128)(2,1)}, u32[]{:S(2)}) copy-start(bf16[1,1,48,600]{3,2,1,0:T(8,128)(2,1)} %param.8) | copy-start | bytes 172804
  4.0 62.9 %all-to-all-start = ((bf16[32,2,3,768]{3,1,2,0:T(2,128)(2,1)}), bf16[32,2,3,768]{3,1,2,0:T(2,128)(2,1)S(1)}, u32[]{:S(2)}, u32[]{:S(2)}) async-start(bf16[32,2,3,768]{3,1,2,0:T(2,128)(2,1)} %broadcast_select_fusion), calls=%async_computation | async-start | bytes 589824 | tf_op jit(solution)/shard_map/all_to_all | solution.py:177
  25.4 0.7 copy-start.4
  25.5 0.7 copy-start.3
  67.8 5.7 %collective-permute-start = (bf16[48,768]{1,0:T(8,128)(2,1)S(1)}, bf16[48,768]{1,0:T(8,128)(2,1)S(1)}, u32[]{:S(2)}, u32[]{:S(2)}) collective-permute-start(bf16[48,768]{1,0:T(8,128)(2,1)S(1)} %broadcast_select_fusion.1), channel_id=1, source_target_pairs={{32,0},{64,32},{96,64},{128,96},{160,128},{192,160},{224,192},{256... | collective-permute-start | bytes 221192 | tf_op jit(solution)/shard_map/ppermute | solution.py:198

commit v2 on v1

--- a/solution.py
+++ b/solution.py
@@ -151,52 +151,272 @@
     )(rowidx, delays, rec, tpl)
 
 
-def normalize(raw):
-    values = raw.astype(jnp.float32)
+MESH = pl.DeviceIdType.MESH
+
+
+def exchange_kernel(
+    plane, cores, picked, cross_at, own_at, own_here, wave_ref, tpl_ref, rec_ref, all_ref,
+    outgoing, arrived, cross, crossed, merged, out_sems, in_sems, pair_sems, halo_sems, line_sems, side_sems
+):
+    tm, spot = lax.axis_index("tm"), lax.axis_index("tmpl")
+    windows = lax.axis_size("tm")
+    chips = windows // cores
+    chip, core = tm // cores, tm % cores
+    half, place = spot // plane, spot % plane
+    other_half = 1 - half
+    partner = other_half * plane + place
+    sibling = chip * cores + (1 - core)
+    channels = wave_ref.shape[1]
+    slots = outgoing.shape[1] // 2
+    table = cross.shape[0] // channels
+    taps = tpl_ref.shape[1]
+
+    barrier = pltpu.get_barrier_semaphore()
+
+    def greet(window, group):
+        pl.semaphore_signal(barrier, inc=1, device_id=(window, group), device_id_type=MESH)
+
+    def near(step, carry):
+        greet(tm, half * plane + (place + step) % plane)
+        return carry
+
+    lax.fori_loop(1, plane, near, 0)
+    greet(tm, partner)
+    greet(sibling, spot)
+
+    @pl.when(chip > 0)
+    def _():
+        greet(tm - cores, spot)
+
+    @pl.when(chip < chips - 1)
+    def _():
+        greet(tm + cores, spot)
+
+    @pl.when((core == 0) & (chip > 0))
+    def _():
+        greet(tm - 1, spot)
+
+    @pl.when((core == 1) & (chip < chips - 1))
+    def _():
+        greet(tm + 1, spot)
+
+    values = tpl_ref[...].astype(jnp.float32)
     centred = values - jnp.mean(values, axis=-1, keepdims=True)
     factor = lax.rsqrt(jnp.sum(centred * centred, axis=-1, keepdims=True) + 1e-06)
-    return (centred * factor).astype(jnp.bfloat16)
-
-
-def fetch_rows(source, group_stations, capacity, own_index):
-    groups, table_size = group_stations.shape
-    station_count = source.shape[0]
+    all_ref[tm] = jnp.zeros(all_ref.shape[1:], all_ref.dtype)
+    all_ref[tm, :, :taps] = (centred * factor).astype(all_ref.dtype)
+
+    def gather(step, carry):
+        for side in range(2):
+            for slot in range(slots):
+                outgoing[step, side * slots + slot] = wave_ref[picked[step, side * slots + slot]]
+        return carry
+
+    lax.fori_loop(0, plane, gather, 0)
+    arrived[place] = outgoing[place]
+
+    after, before = (chip + chips - 1) // chips, (2 * chips - 2 - chip) // chips
+    pl.semaphore_wait(barrier, plane + 1 + after * (2 - core) + before * (1 + core))
+
+    def row_copy(step):
+        to = (place + step) % plane
+        return pltpu.make_async_remote_copy(
+            src_ref=outgoing.at[to], dst_ref=arrived.at[place],
+            send_sem=out_sems.at[step], recv_sem=in_sems.at[step],
+            device_id=(tm, half * plane + to), device_id_type=MESH,
+        )
+
+    def line_copy(way, step):
+        window = tm - way * cores * step
+        lane = (1 - way) // 2
+        return pltpu.make_async_remote_copy(
+            src_ref=all_ref.at[window], dst_ref=all_ref.at[window],
+            send_sem=line_sems.at[lane, 0, step], recv_sem=line_sems.at[lane, 1, step],
+            device_id=(tm + way * cores, spot), device_id_type=MESH,
+        )
+
+    def side_copy(way, step):
+        window = tm - way * cores * step
+        lane = (1 - way) // 2
+        return pltpu.make_async_remote_copy(
+            src_ref=all_ref.at[window], dst_ref=all_ref.at[window],
+            send_sem=side_sems.at[lane, 0, step], recv_sem=side_sems.at[lane, 1, step],
+            device_id=(sibling, spot), device_id_type=MESH,
+        )
+
+    def can_send(way):
+        return chip < chips - 1 if way == 1 else chip > 0
+
+    def holds(way, step):
+        return chip >= step if way == 1 else chip + step <= chips - 1
+
+    for way in (1, -1):
+        @pl.when(can_send(way))
+        def _(way=way):
+            line_copy(way, 0).start()
+
+    def send_rows(step, carry):
+        row_copy(step).start()
+        return carry
+
+    lax.fori_loop(1, plane, send_rows, 0)
+    side_copy(1, 0).start()
+
+    def relay(step):
+        for way in (1, -1):
+            @pl.when(holds(way, step))
+            def _(way=way):
+                line_copy(way, step - 1).wait_recv()
+                @pl.when(can_send(way))
+                def _():
+                    line_copy(way, step).start()
+                side_copy(way, step).start()
+
+    relay(1)
+
+    def take_rows(step, carry):
+        row_copy(step).wait_recv()
+        return carry
+
+    lax.fori_loop(1, plane, take_rows, 0)
+
+    for k in range(table):
+        merged[channels * k : channels * (k + 1), :] = arrived[cross_at[k, 0], cross_at[k, 1]].astype(jnp.float32)
+    cross[...] = merged[...].astype(cross.dtype)
+    pair = pltpu.make_async_remote_copy(
+        src_ref=cross, dst_ref=crossed, send_sem=pair_sems.at[0], recv_sem=pair_sems.at[1],
+        device_id=(tm, partner), device_id_type=MESH,
+    )
+    pair.start()
+
+    relay(2)
+    relay(3)
+    pair.wait_recv()
+    far = crossed[...].astype(jnp.float32)
+    for k in range(table):
+        here = arrived[own_at[k, 0], own_at[k, 1]].astype(jnp.float32)
+        merged[channels * k : channels * (k + 1), :] = jnp.where(
+            own_here[k] == 1, here, far[channels * k : channels * (k + 1)]
+        )
+    rec_ref[0] = merged[...].astype(rec_ref.dtype)
+
+    halo = pltpu.make_async_remote_copy(
+        src_ref=rec_ref.at[0], dst_ref=rec_ref.at[1], send_sem=halo_sems.at[0], recv_sem=halo_sems.at[1],
+        device_id=((tm + windows - 1) % windows, spot), device_id_type=MESH,
+    )
+
+    @pl.when(tm > 0)
+    def _():
+        halo.start()
+
+    for step in range(4, chips):
+        relay(step)
+
+    @pl.when(tm == windows - 1)
+    def _():
+        rec_ref[1] = jnp.zeros(rec_ref.shape[1:], rec_ref.dtype)
+
+    @pl.when(tm < windows - 1)
+    def _():
+        halo.wait_recv()
+
+    side_copy(1, 0).wait()
+    for step in range(1, chips):
+        for way in (1, -1):
+            @pl.when(holds(way, step))
+            def _(way=way, step=step):
+                side_copy(way, step).wait()
+    for step in range(chips - 1):
+        for way in (1, -1):
+            @pl.when(holds(way, step) & can_send(way))
+            def _(way=way, step=step):
+                line_copy(way, step).wait_send()
+
+    def sent_rows(step, carry):
+        row_copy(step).wait_send()
+        return carry
+
+    lax.fori_loop(1, plane, sent_rows, 0)
+    pair.wait_send()
+
+    @pl.when(tm > 0)
+    def _():
+        halo.wait_send()
+
+
+def exchange(wave, tpl, picked, cross_at, own_at, own_here, padded):
+    windows = lax.axis_size("tm")
+    plane = picked.shape[0]
+    cores = 2
+    channels, samples = wave.shape[1:]
+    table = own_here.shape[0]
+    nrc = table * channels
+    vm = pl.BlockSpec(memory_space=pltpu.VMEM)
+    sm = pl.BlockSpec(memory_space=pltpu.SMEM)
+    chips = windows // cores
+    return pl.pallas_call(
+        functools.partial(exchange_kernel, plane, cores),
+        out_shape=(
+            jax.ShapeDtypeStruct((2, nrc, samples), jnp.bfloat16),
+            jax.ShapeDtypeStruct((windows, tpl.shape[0], padded), jnp.bfloat16),
+        ),
+        in_specs=[sm] * 4 + [vm] * 2,
+        out_specs=(vm, vm),
+        scratch_shapes=[
+            pltpu.VMEM((plane, picked.shape[1], channels, samples), jnp.bfloat16),
+            pltpu.VMEM((plane, picked.shape[1], channels, samples), jnp.bfloat16),
+            pltpu.VMEM((nrc, samples), jnp.bfloat16),
+            pltpu.VMEM((nrc, samples), jnp.bfloat16),
+            pltpu.VMEM((nrc, samples), jnp.float32),
+            pltpu.SemaphoreType.DMA((plane,)),
+            pltpu.SemaphoreType.DMA((plane,)),
+            pltpu.SemaphoreType.DMA((2,)),
+            pltpu.SemaphoreType.DMA((2,)),
+            pltpu.SemaphoreType.DMA((2, 2, chips)),
+            pltpu.SemaphoreType.DMA((2, 2, chips)),
+        ],
+        compiler_params=pltpu.CompilerParams(
+            collective_id=0, has_side_effects=True, vmem_limit_bytes=32 << 20
+        ),
+    )(picked, cross_at, own_at, own_here, wave, tpl)
+
+
+def routes(group_stations, station_count, plane, capacity):
+    spot = lax.axis_index("tmpl")
+    half, place = spot // plane, spot % plane
     owners = group_stations // station_count
-    row_local = group_stations % station_count
-    position = jnp.arange(table_size, dtype=jnp.int32)
-    same_owner = owners[:, :, None] == owners[:, None, :]
+    locals_ = group_stations % station_count
+    table = group_stations.shape[1]
+    position = jnp.arange(table, dtype=jnp.int32)
+    same = owners[:, :, None] == owners[:, None, :]
     earlier = position[:, None] > position[None, :]
-    owner_rank = jnp.sum((same_owner & earlier[None]).astype(jnp.int32), axis=2)
-    slot_ids = jnp.arange(capacity, dtype=jnp.int32)
-    matched = (owners[:, :, None] == own_index) & (
-        owner_rank[:, :, None] == slot_ids[None, None, :]
-    )
-    picked = jnp.sum(jnp.where(matched, row_local[:, :, None], 0), axis=1)
-    outgoing = jnp.take(source, picked.reshape(-1), axis=0)
-    outgoing = outgoing.reshape(groups, capacity, source.shape[1], source.shape[2])
-    incoming = lax.all_to_all(outgoing, "tmpl", split_axis=0, concat_axis=0, tiled=True)
-    arrived = incoming.reshape(groups * capacity, source.shape[1], source.shape[2])
-    mine_owner = jnp.take(owners, own_index, axis=0)
-    mine_rank = jnp.take(owner_rank, own_index, axis=0)
-    return jnp.take(arrived, mine_owner * capacity + mine_rank, axis=0)
+    rank = jnp.sum((same & earlier[None]).astype(jnp.int32), axis=2)
+    slots = jnp.arange(capacity, dtype=jnp.int32)
+    matched = (owners == spot)[:, :, None] & (rank[:, :, None] == slots)
+    picked = jnp.sum(jnp.where(matched, locals_[:, :, None], 0), axis=1)
+    picked = picked.reshape(2, plane, capacity).transpose(1, 0, 2).reshape(plane, 2 * capacity)
+
+    def found(group, side):
+        mine = lax.dynamic_index_in_dim(owners, group, 0, keepdims=False)
+        order = lax.dynamic_index_in_dim(rank, group, 0, keepdims=False)
+        return jnp.stack([mine % plane, side * capacity + order], axis=1), mine // plane == half
+
+    cross_at, _ = found((1 - half) * plane + place, 1 - half)
+    own_at, own_here = found(spot, half)
+    return picked, cross_at, own_at, own_here.astype(jnp.int32)
 
 
 def per_device(waveforms, templates, group_stations, template_rows, moveouts):
     groups = lax.axis_size("tmpl")
-    windows = lax.axis_size("tm")
-    own_index = lax.axis_index("tmpl")
-    channels, samples = waveforms.shape[1:]
+    station_count, channels, samples = waveforms.shape
     table_size = group_stations.shape[1]
     capacity = max(2, 2 * table_size // groups)
     taps = templates.shape[3]
     padded = (taps + LANES - 1) // LANES * LANES
-    normed = normalize(templates[0, 0])
-    normed = jnp.pad(normed, ((0, 0), (0, padded - taps)))
-    tpl = lax.all_gather(normed, "tm", axis=0, tiled=True)
-    rows = fetch_rows(waveforms, group_stations, capacity, own_index)
-    rows = rows.reshape(table_size * channels, samples)
-    later = lax.ppermute(rows, "tm", [(w, w - 1) for w in range(1, windows)])
-    rec = jnp.concatenate([rows, later], axis=0)
+    picked, cross_at, own_at, own_here = routes(group_stations, station_count, groups // 2, capacity)
+    rec, tpl = exchange(waveforms, templates[0, 0], picked, cross_at, own_at, own_here, padded)
+    rec = rec.reshape(-1, samples)
+    tpl = tpl.reshape(-1, padded)
     lists, shifts = template_rows[0], moveouts[0]
     tpls, per_template = lists.shape
     hit = lists[:, :, None] == jnp.arange(table_size, dtype=jnp.int32)

time: 89.4 us -> 69 us (0.77)
  Pallas kernels: 15.4 us -> 64.7 us
  blocking collectives: 39.9 us -> 0 us
  starting transfers between devices: 23.3 us -> 0 us
  waiting for transfers between devices: 3.52 us -> 0 us
  other arithmetic: 2.84 us -> 0.56 us
    pallas_call x0 -> x1, Pallas kernels: none -> 49.2 us  [exchange(): pl.pallas_call(functools.partial(exchange_kernel, plane, cores), out_shap...]
    all_gather x1 -> x0, blocking collectives: 39.9 us -> none  [per_device(): tpl = lax.all_gather(normed, 'tm', axis=0, tiled=True)]
    all_to_all x1 -> x0, starting transfers between devices: 21.3 us -> none  [fetch_rows(): lax.all_to_all(outgoing, 'tmpl', split_axis=0, concat_axis=0, tiled=True)]
    ppermute x1 -> x0, waiting for transfers between devices: 3.51 us -> none  [per_device(): later = lax.ppermute(rows, 'tm', [(w, w - 1) for w in range(1, windows)])]
    gather x4 -> x0, local copies, waits for them, and re-layouts: 2.29 us -> none  [the longest x2 1.59 us: fetch_rows(): outgoing = jnp.take(source, picked.reshape(-1), axis=0)]
    unnamed x10 -> x9, local copies, waits for them, and re-layouts: 0.69 us -> 2.79 us
    select_n x5 -> x2, other arithmetic: 2.09 us -> 0.02 us  [the longest x1 0.01 us: routes(): locals_ = group_stations % station_count]
    ppermute x1 -> x0, starting transfers between devices: 2.06 us -> none  [per_device(): later = lax.ppermute(rows, 'tm', [(w, w - 1) for w in range(1, windows)])]
  transfers between devices with their start and end apart: 2 -> 0, of which waited for: 1 -> 0; matrix products, arithmetic and copies ran while one was open for 1% -> 0% of each run, Pallas kernels for 0% -> 0%
where the time goes in v2:
time: 69 us; the launch traced here: 68.8 us
  Pallas kernels  64.7 us (94%)
  local copies, waits for them, and re-layouts  3.46 us (5%)
    pallas_call x1, Pallas kernels, exchange(): pl.pallas_call(functools.partial(exchange_kernel, plane, cores), out_shap...  49.2 us
    pallas_call x1, Pallas kernels, correlate(): pl.pallas_call(functools.partial(correlate_kernel, taps), out_shape=jax.S...  15.4 us
    unnamed x9, local copies, waits for them, and re-layouts  2.79 us

profile of v2, /device:TPU:1, one launch (start us, length us, event | category | flops | bytes accessed | tf_op | source)
XLA Modules:
  0.0 68.8 jit_solution(18244501043656311267)
XLA Ops:
  0.0 0.0 copy-start.1
  0.0 0.7 %copy-done.1 = s32[32,16]{0,1:T(8,128)S(1)} copy-done((s32[32,16]{0,1:T(8,128)S(1)}, s32[32,16]{0,1:T(8,128)}, u32[]{:S(2)}) %copy-start.1) | copy-done | bytes 2072
  0.7 0.2 dynamic-slice_reduce_fusion
  1.0 0.1 convert_reduce_fusion
  1.1 0.2 add_reduce_fusion
  1.3 0.1 copy.57.own_at
  1.4 0.1 copy.56.cross_at
  1.5 0.1 reshape.164
  1.6 0.1 copy.55.picked
  1.7 0.0 copy-start
  1.7 1.4 %copy.58.wave_ref = bf16[96,3,768]{2,1,0:T(4,128)(2,1)S(1)} copy(bf16[96,3,768]{2,0,1:T(8,128)(2,1)} %param.5) | data formatting | bytes 884736 | tf_op args[0]
  3.1 0.0 copy-done
  3.1 0.0 copy-start.3
  3.1 49.2 %shard_map.55 = (bf16[2,48,768]{2,1,0:T(8,128)(2,1)S(1)}, bf16[16,48,640]{2,1,0:T(8,128)(2,1)S(1)}) custom-call(s32[16,4]{1,0:T(8,128)S(1)} %copy.55.picked, s32[16,2]{1,0:T(8,128)S(1)} %copy.56.cross_at, s32[16,2]{1,0:T(8,128)S(1)} %copy.57.own_at, s32[16]{0:T(128)S(1)} %compare_convert_fusion.own_here, bf16[96,3,768]{2,1,0:T(4,128)(2,1)S(1)} %copy.58.wave_ref, ...), custom_call_target="tpu_custom_call" | custom-call | tf_op jit(solution)/shard_map/pallas_call | solution.py:357
  52.3 0.0 copy-start.2
  52.4 0.0 copy-done.3
  52.4 0.7 copy-done.2
  53.0 0.1 select_reduce_fusion
  53.2 0.1 copy.52
  53.3 0.1 copy.53
  53.3 15.4 %shard_map.56 = f32[16,768]{1,0:T(8,128)} custom-call(s32[16,16]{1,0:T(8,128)S(1)} %add_bitcast_fusion.rowidx, s32[16,16]{1,0:T(8,128)S(1)} %bitcast.22, bf16[96,768]{1,0:T(8,128)(2,1)S(1)} %bitcast.20, bf16[768,640]{1,0:T(8,128)(2,1)S(1)} %bitcast.19), custom_call_target="tpu_custom_call" | custom-call | tf_op jit(solution)/shard_map/pallas_call | solution.py:136
  (11 shorter events, 0.1 us)
Async XLA Ops:
  0.0 0.7 %copy-start.1 = (s32[32,16]{0,1:T(8,128)S(1)}, s32[32,16]{0,1:T(8,128)}, u32[]{:S(2)}) copy-start(s32[32,16]{0,1:T(8,128)} %param.7) | copy-start | bytes 6148
  1.7 1.4 %copy-start = (bf16[1,1,48,600]{3,2,1,0:T(8,128)(2,1)S(1)}, bf16[1,1,48,600]{3,2,1,0:T(8,128)(2,1)}, u32[]{:S(2)}) copy-start(bf16[1,1,48,600]{3,2,1,0:T(8,128)(2,1)} %param.6) | copy-start | bytes 172804
  3.1 49.3 %copy-start.3 = (s32[1,16,16]{2,1,0:T(8,128)S(1)}, s32[1,16,16]{2,1,0:T(8,128)}, u32[]{:S(2)}) copy-start(s32[1,16,16]{2,1,0:T(8,128)} %param.8) | copy-start | bytes 3076
  52.3 0.7 %copy-start.2 = (s32[1,16,16]{2,1,0:T(8,128)S(1)}, s32[1,16,16]{2,1,0:T(8,128)}, u32[]{:S(2)}) copy-start(s32[1,16,16]{2,1,0:T(8,128)} %param.9) | copy-start | bytes 3076

commit v3 on v1

v3 whole, which is shorter than its diff:
```python
import functools

import jax
import jax.numpy as jnp
from jax import lax
from jax.experimental import pallas as pl
from jax.experimental.pallas import tpu as pltpu
from jax.sharding import PartitionSpec as P

STRIDE = 8
LANES = 128


def iota(shape, dim):
    return lax.broadcasted_iota(jnp.int32, shape, dim)


def correlate_kernel(
    taps, lists, shifts, near_ref, far_ref, tpl_ref, out_ref, rowidx, delays, tplf, xa, xb, inv, zs, ws, acc
):
    stations, tpls = rowidx.shape
    nrc = xa.shape[0]
    channels = nrc // stations
    samples = near_ref.shape[2]
    frames = samples // STRIDE
    padded = tpl_ref.shape[2]
    kblocks = padded // LANES
    groups = taps // STRIDE + 1
    lane = iota((STRIDE, LANES), 1)
    sub = iota((STRIDE, LANES), 0)

    def use(t, carry):
        for k in range(lists.shape[2]):
            station = lists[0, t, k]
            rowidx[station, t] = t * nrc + k * channels
            delays[station, t] = shifts[0, t, k]
        return carry

    lax.fori_loop(0, tpls, use, 0)
    for t in range(tpls):
        tplf[t * nrc : (t + 1) * nrc, :] = tpl_ref[t].astype(jnp.float32)
    record = (near_ref[...].astype(jnp.float32) + far_ref[...].astype(jnp.float32)).astype(jnp.bfloat16)
    record = record.reshape(2 * nrc, samples)

    gap = iota((samples, LANES), 0) - STRIDE * iota((samples, LANES), 1)
    flat_lane = iota((nrc, LANES), 1)
    for e in range(STRIDE):
        pick = jnp.where(gap == e, 1.0, 0.0).astype(jnp.bfloat16)
        phase = jnp.dot(record, pick, preferred_element_type=jnp.float32)
        later = pltpu.roll(phase[nrc:], frames, axis=1)
        xa[:, e, :] = jnp.where(flat_lane < frames, phase[:nrc], later)
        xb[:, e, :] = later

    ahead = iota((2 * LANES, LANES), 0) - iota((2 * LANES, LANES), 1)
    band = jnp.where((ahead >= 0) & (ahead < taps // STRIDE), 1.0, 0.0).astype(jnp.bfloat16)
    flat = jnp.concatenate([xa[...].reshape(nrc * STRIDE, LANES), xb[...].reshape(nrc * STRIDE, LANES)], axis=1)
    square = flat * flat
    high = square.astype(jnp.bfloat16)
    low = (square - high.astype(jnp.float32)).astype(jnp.bfloat16)

    def banded(v):
        return jnp.dot(v, band, preferred_element_type=jnp.float32)

    def octet(v):
        v = v.reshape(nrc, STRIDE, LANES)
        row = iota((nrc, STRIDE, LANES), 1)
        for k in (1, 2, 4):
            nxt = pltpu.roll(v, LANES - 1, axis=2)
            v = v + pltpu.roll(jnp.where(row < k, nxt, v), STRIDE - k, axis=1)
        return v

    wsum = octet(banded(flat.astype(jnp.bfloat16)))
    wsq = octet(banded(high) + banded(low))
    inv[...] = lax.rsqrt(jnp.maximum(wsq - wsum * wsum / taps, 1.0))

    acc[...] = jnp.zeros_like(acc)
    for i in range(groups, padded // STRIDE, 2):
        for c in range(channels):
            for slot in range(2):
                zs[slot, c, STRIDE * i : STRIDE * (i + 2), :] = jnp.zeros((2 * STRIDE, LANES), jnp.bfloat16)

    def build(r, slot):
        for c in range(channels):
            rc = r * channels + c
            a, b = xa[rc], xb[rc]
            for i in range(0, groups, 2):
                pair = [
                    pltpu.roll(jnp.where(lane < s, b, a), (LANES - s) % LANES, axis=1) for s in (i, i + 1)
                ]
                zs[slot, c, STRIDE * i : STRIDE * (i + 2), :] = jnp.concatenate(pair, axis=0).astype(jnp.bfloat16)
            for t in range(0, tpls, 2):
                rolled = []
                for tt in (t, t + 1):
                    row = tplf[pl.ds(rowidx[r, tt] + c, 1), :]
                    rolled.append([
                        pltpu.roll(
                            jnp.broadcast_to(row[:, LANES * k : LANES * (k + 1)], (STRIDE, LANES)),
                            0, axis=1, stride=1, stride_axis=0,
                        )
                        for k in range(kblocks)
                    ])
                for k in range(kblocks):
                    both = [
                        jnp.where(lane < sub, p[k - 1] if k else jnp.zeros_like(p[0]), p[k]) for p in rolled
                    ]
                    ws[slot, c, STRIDE * t : STRIDE * (t + 2), LANES * k : LANES * (k + 1)] = jnp.concatenate(
                        both, axis=0
                    ).astype(jnp.bfloat16)

    def multiply(slot):
        return [jnp.dot(ws[slot, c], zs[slot, c], preferred_element_type=jnp.float32) for c in range(channels)]

    def settle(r, products):
        ratio = sum(
            products[c].reshape(tpls, STRIDE, LANES) * inv[r * channels + c][None] for c in range(channels)
        )
        for t in range(tpls):
            m = delays[r, t]
            f = m // STRIDE
            e = m - f * STRIDE
            near = pltpu.roll(ratio[t], (LANES - f) % LANES, axis=1)
            far = pltpu.roll(near, LANES - 1, axis=1)
            acc[t] += pltpu.roll(jnp.where(sub < e, far, near), (STRIDE - e) % STRIDE, axis=0)

    build(0, 0)

    def pair_of(p, carry):
        first = 2 * p
        products = multiply(0)
        build(first + 1, 1)
        settle(first, products)
        products = multiply(1)
        build(jnp.minimum(first + 2, stations - 1), 0)
        settle(first + 1, products)
        return carry

    lax.fori_loop(0, stations // 2, pair_of, 0)

    total = acc[...].reshape(tpls * STRIDE, LANES)
    p1 = total.astype(jnp.bfloat16)
    rest = total - p1.astype(jnp.float32)
    p2 = rest.astype(jnp.bfloat16)
    p3 = (rest - p2.astype(jnp.float32)).astype(jnp.bfloat16)
    spots = iota((LANES, samples), 1) // STRIDE
    spread_out = jnp.where(spots == iota((LANES, samples), 0), 1.0, 0.0).astype(jnp.bfloat16)

    def placed(v):
        return jnp.dot(v, spread_out, preferred_element_type=jnp.float32)

    wide = (placed(p1) + placed(p2) + placed(p3)).reshape(tpls, STRIDE, samples)
    mine = iota((tpls, STRIDE, samples), 2) % STRIDE == iota((tpls, STRIDE, samples), 1)
    out_ref[...] = jnp.sum(jnp.where(mine, wide, 0.0), axis=1)


def correlate(near, far, tpl, lists, shifts, taps):
    samples = near.shape[2]
    tpls, nrc, padded = tpl.shape
    stations = lists.shape[2]
    channels = nrc // stations
    vm = pl.BlockSpec(memory_space=pltpu.VMEM)
    sm = pl.BlockSpec(memory_space=pltpu.SMEM)
    return pl.pallas_call(
        functools.partial(correlate_kernel, taps),
        out_shape=jax.ShapeDtypeStruct((tpls, samples), jnp.float32),
        in_specs=[sm, sm, vm, vm, vm],
        out_specs=vm,
        scratch_shapes=[
            pltpu.SMEM((stations, tpls), jnp.int32),
            pltpu.SMEM((stations, tpls), jnp.int32),
            pltpu.VMEM((tpls * nrc, padded), jnp.float32),
            pltpu.VMEM((nrc, STRIDE, LANES), jnp.float32),
            pltpu.VMEM((nrc, STRIDE, LANES), jnp.float32),
            pltpu.VMEM((nrc, STRIDE, LANES), jnp.float32),
            pltpu.VMEM((2, channels, padded, LANES), jnp.bfloat16),
            pltpu.VMEM((2, channels, tpls * STRIDE, padded), jnp.bfloat16),
            pltpu.VMEM((tpls, STRIDE, LANES), jnp.float32),
        ],
        compiler_params=pltpu.CompilerParams(vmem_limit_bytes=32 << 20),
    )(lists, shifts, near, far, tpl)


MESH = pl.DeviceIdType.MESH
REACH = 2
EARLY = (2,)
ORDER = (1, 4, 3, 6, 5, 7)


def exchange_kernel(
    plane, cores, slots, table_hbm, wave_hbm, tpl_hbm, near_ref, far_ref, all_ref,
    table, wave, raw, picked, chosen, outgoing, arrived, cross,
    load_sems, out_sems, in_sems, pair_sems, halo_sems, line_sends, line_recvs, side_sends, side_recvs
):
    tm, spot = lax.axis_index("tm"), lax.axis_index("tmpl")
    windows = lax.axis_size("tm")
    chips = windows // cores
    chip, core = tm // cores, tm % cores
    half, place = spot // plane, spot % plane
    partner = (1 - half) * plane + place
    sibling = chip * cores + (1 - core)
    channels, stored, samples = wave.shape
    stations, groups = table.shape
    unit = arrived.shape[1]
    taps = raw.shape[1]

    loads = [
        pltpu.make_async_copy(src, dst, load_sems.at[n])
        for n, (src, dst) in enumerate([(table_hbm, table), (wave_hbm, wave), (tpl_hbm, raw)])
    ]
    for load in loads:
        load.start()

    barrier = pltpu.get_barrier_semaphore()

    def greet(window, group):
        pl.semaphore_signal(barrier, inc=1, device_id=(window, group), device_id_type=MESH)

    def room(way):
        return chips - 1 - chip if way == 1 else chip

    def greet_plane(step, carry):
        greet(tm, half * plane + (place + step) % plane)
        return carry

    greet(tm, partner)
    lax.fori_loop(1, plane, greet_plane, 0)
    for step in range(1, REACH + 1):
        for way in (1, -1):
            @pl.when(room(way) >= step)
            def _(way=way, step=step):
                greet(tm + way * cores * step, spot)
    greet(sibling, spot)

    @pl.when((core == 0) & (chip > 0))
    def _():
        greet(tm - 1, spot)

    @pl.when((core == 1) & (chip < chips - 1))
    def _():
        greet(tm + 1, spot)

    loads[0].wait()
    base = spot * stored

    def scan(group, carry):
        count = 0
        found = [0] * slots
        for k in range(stations):
            gap = table[k, group] - base
            hit = (gap >= 0) & (gap < stored)
            found = [jnp.where(hit & (count == n), gap, found[n]) for n in range(slots)]
            count = count + jnp.where(hit, 1, 0)
        for n in range(slots):
            picked[group % plane, (group // plane) * slots + n] = found[n]
        return carry

    lax.fori_loop(0, groups, scan, 0)
    loads[1].wait()

    row = iota((unit, channels * stored), 0)
    column = iota((unit, channels * stored), 1)

    def choose(step, carry):
        want = jnp.where(row < 2 * slots * channels, row % channels * stored, -stored)
        for n in range(2 * slots):
            want = want + jnp.where(row // channels == n, picked[step, n], 0)
        chosen[pl.ds(pl.multiple_of(step * unit, unit), unit), :] = jnp.where(column == want, 1.0, 0.0).astype(chosen.dtype)
        return carry

    lax.fori_loop(0, plane, choose, 0)
    outgoing[...] = jnp.dot(
        chosen[...], wave[...].reshape(channels * stored, samples), preferred_element_type=jnp.float32
    ).astype(outgoing.dtype).reshape(outgoing.shape)
    arrived[place] = outgoing[place]

    spots = iota((stations * channels, plane * unit), 0)
    order = iota((stations * channels, plane * unit), 1)

    def collect(group, side):
        want = spots % channels
        owners = []
        for k in range(stations):
            station = table[k, group]
            owner = station // stored
            rank = 0
            for earlier in owners:
                rank = rank + jnp.where(earlier == owner, 1, 0)
            owners.append(owner)
            place_of = owner % plane * unit + (side * slots + rank) * channels
            place_of = jnp.where(owner // plane == half, place_of, -channels)
            want = want + jnp.where(spots // channels == k, place_of, 0)
        return jnp.where(order == want, 1.0, 0.0).astype(arrived.dtype)

    across = collect(partner, 1 - half)
    local = collect(spot, half)

    loads[2].wait()
    values = raw[...].astype(jnp.float32)
    centred = values - jnp.mean(values, axis=-1, keepdims=True)
    factor = lax.rsqrt(jnp.sum(centred * centred, axis=-1, keepdims=True) + 1e-06)
    all_ref[tm] = jnp.zeros(all_ref.shape[1:], all_ref.dtype)
    all_ref[tm, :, :taps] = (centred * factor).astype(all_ref.dtype)

    peers = plane + 1
    for step in range(1, REACH + 1):
        for way in (1, -1):
            peers = peers + (room(way) + chips - step) // chips
    peers = peers + (1 - core) * ((chip + chips - 1) // chips) + core * ((2 * chips - 2 - chip) // chips)
    pl.semaphore_wait(barrier, peers)

    def row_copy(step):
        to = (place + step) % plane
        return pltpu.make_async_remote_copy(
            src_ref=outgoing.at[to], dst_ref=arrived.at[place],
            send_sem=out_sems.at[step], recv_sem=in_sems.at[step],
            device_id=(tm, half * plane + to), device_id_type=MESH,
        )

    def line_copy(way, come, go):
        window = tm - way * cores * come
        lane = (1 - way) // 2
        return pltpu.make_async_remote_copy(
            src_ref=all_ref.at[window], dst_ref=all_ref.at[window],
            send_sem=line_sends.at[lane, come + go], recv_sem=line_recvs.at[lane, come + go],
            device_id=(tm + way * cores * go, spot), device_id_type=MESH,
        )

    def side_copy(way, come):
        window = tm - way * cores * come
        lane = (1 - way) // 2
        return pltpu.make_async_remote_copy(
            src_ref=all_ref.at[window], dst_ref=all_ref.at[window],
            send_sem=side_sends.at[lane, come], recv_sem=side_recvs.at[lane, come],
            device_id=(sibling, spot), device_id_type=MESH,
        )

    def send_rows(step, carry):
        row_copy(step).start()
        return carry

    def take_rows(step, carry):
        row_copy(step).wait_recv()
        return carry

    def sent_rows(step, carry):
        row_copy(step).wait_send()
        return carry

    lax.fori_loop(1, plane, send_rows, 0)
    for go in range(REACH, 0, -1):
        for way in (1, -1):
            @pl.when(room(way) >= go)
            def _(way=way, go=go):
                line_copy(way, 0, go).start()
    side_copy(1, 0).start()

    def receive(come):
        for way in (1, -1):
            @pl.when(room(-way) >= come)
            def _(way=way):
                line_copy(way, come, 0).wait_recv()
                if come % REACH == 0:
                    for go in range(min(REACH, chips - 1 - come), 0, -1):
                        @pl.when(room(way) >= go)
                        def _(go=go):
                            line_copy(way, come, go).start()
                side_copy(way, come).start()

    for come in EARLY:
        receive(come)
    lax.fori_loop(1, plane, take_rows, 0)

    def pull(hot):
        rows = arrived[...].reshape(plane * unit, samples)
        return jnp.dot(hot, rows, preferred_element_type=jnp.float32).astype(arrived.dtype)

    cross[...] = pull(across)
    pair = pltpu.make_async_remote_copy(
        src_ref=cross, dst_ref=far_ref.at[0], send_sem=pair_sems.at[0], recv_sem=pair_sems.at[1],
        device_id=(tm, partner), device_id_type=MESH,
    )
    pair.start()
    near_ref[0] = pull(local)

    def halo(n):
        ref = (near_ref, far_ref)[n]
        return pltpu.make_async_remote_copy(
            src_ref=ref.at[0], dst_ref=ref.at[1], send_sem=halo_sems.at[n, 0], recv_sem=halo_sems.at[n, 1],
            device_id=((tm + windows - 1) % windows, spot), device_id_type=MESH,
        )

    @pl.when(tm > 0)
    def _():
        halo(0).start()

    @pl.when(tm == windows - 1)
    def _():
        near_ref[1] = jnp.zeros(near_ref.shape[1:], near_ref.dtype)
        far_ref[1] = jnp.zeros(far_ref.shape[1:], far_ref.dtype)

    for come in ORDER:
        receive(come)

    pair.wait_recv()

    @pl.when(tm > 0)
    def _():
        halo(1).start()

    side_copy(1, 0).wait()
    for come in range(1, chips):
        for way in (1, -1):
            @pl.when(room(-way) >= come)
            def _(way=way, come=come):
                side_copy(way, come).wait()
    for come in range(0, chips, REACH):
        for go in range(1, min(REACH, chips - 1 - come) + 1):
            for way in (1, -1):
                @pl.when((room(-way) >= come) & (room(way) >= go))
                def _(way=way, come=come, go=go):
                    line_copy(way, come, go).wait_send()
    lax.fori_loop(1, plane, sent_rows, 0)
    pair.wait_send()

    @pl.when(tm < windows - 1)
    def _():
        halo(0).wait_recv()
        halo(1).wait_recv()

    @pl.when(tm > 0)
    def _():
        halo(0).wait_send()
        halo(1).wait_send()


def exchange(table, wave, tpl, slots, padded):
    windows = lax.axis_size("tm")
    cores = 2
    stations, groups = table.shape
    plane = groups // 2
    channels, stored, samples = wave.shape
    unit = -(-2 * slots * channels // 8) * 8
    nrc = stations * channels
    vm = pl.BlockSpec(memory_space=pltpu.VMEM)
    hbm = pl.BlockSpec(memory_space=pltpu.HBM)
    chips = windows // cores
    record = jax.ShapeDtypeStruct((2, nrc, samples), jnp.bfloat16)
    return pl.pallas_call(
        functools.partial(exchange_kernel, plane, cores, slots),
        out_shape=(record, record, jax.ShapeDtypeStruct((windows, tpl.shape[0], padded), jnp.bfloat16)),
        in_specs=[hbm] * 3,
        out_specs=(vm, vm, vm),
        scratch_shapes=[
            pltpu.SMEM(table.shape, jnp.int32),
            pltpu.VMEM(wave.shape, wave.dtype),
            pltpu.VMEM(tpl.shape, tpl.dtype),
            pltpu.SMEM((plane, 2 * slots), jnp.int32),
            pltpu.VMEM((plane * unit, channels * stored), jnp.bfloat16),
            pltpu.VMEM((plane, unit, samples), jnp.bfloat16),
            pltpu.VMEM((plane, unit, samples), jnp.bfloat16),
            pltpu.VMEM((nrc, samples), jnp.bfloat16),
            pltpu.SemaphoreType.DMA((3,)),
            pltpu.SemaphoreType.DMA((plane,)),
            pltpu.SemaphoreType.DMA((plane,)),
            pltpu.SemaphoreType.DMA((2,)),
            pltpu.SemaphoreType.DMA((2, 2)),
            pltpu.SemaphoreType.DMA((2, chips)),
            pltpu.SemaphoreType.DMA((2, chips)),
            pltpu.SemaphoreType.DMA((2, chips)),
            pltpu.SemaphoreType.DMA((2, chips)),
        ],
        compiler_params=pltpu.CompilerParams(
            collective_id=0, has_side_effects=True, vmem_limit_bytes=32 << 20
        ),
    )(table, wave, tpl)


def per_device(waveforms, templates, group_stations, template_rows, moveouts):
    table_size = group_stations.shape[1]
    slots = max(2, 2 * table_size // lax.axis_size("tmpl"))
    taps = templates.shape[3]
    padded = (taps + LANES - 1) // LANES * LANES
    near, far, tpl = exchange(
        group_stations.T, waveforms.transpose(1, 0, 2), templates[0, 0], slots, padded
    )
    return correlate(near, far, tpl, template_rows, moveouts, taps)[None]


def solution(mesh):
    in_specs = (
        P("tmpl", None, "tm"),
        P("tmpl", "tm", None, None),
        P(),
        P("tmpl", None, None),
        P("tmpl", None, None),
    )
    out_specs = P("tmpl", None, "tm")
    return jax.shard_map(
        per_device, mesh=mesh, in_specs=in_specs, out_specs=out_specs, check_vma=False
    )
```

time: 89.4 us -> 56.6 us (0.63)
  blocking collectives: 39.9 us -> 0 us
  Pallas kernels: 15.4 us -> 53.7 us
  starting transfers between devices: 23.3 us -> 0 us
  waiting for transfers between devices: 3.52 us -> 0 us
  other arithmetic: 2.84 us -> 0 us
  local copies, waits for them, and re-layouts: 3.75 us -> 2.54 us
    pallas_call x0 -> x1, Pallas kernels: none -> 41.2 us  [exchange(): pl.pallas_call(functools.partial(exchange_kernel, plane, cores, slots), o...]
    all_gather x1 -> x0, blocking collectives: 39.9 us -> none  [per_device(): tpl = lax.all_gather(normed, 'tm', axis=0, tiled=True)]
    all_to_all x1 -> x0, starting transfers between devices: 21.3 us -> none  [fetch_rows(): lax.all_to_all(outgoing, 'tmpl', split_axis=0, concat_axis=0, tiled=True)]
    ppermute x1 -> x0, waiting for transfers between devices: 3.51 us -> none  [per_device(): later = lax.ppermute(rows, 'tm', [(w, w - 1) for w in range(1, windows)])]
    pallas_call x1, Pallas kernels: 15.4 us -> 12.5 us  [correlate(): pl.pallas_call(functools.partial(correlate_kernel, taps), out_shape=jax.S...]
    gather x4 -> x0, local copies, waits for them, and re-layouts: 2.29 us -> none  [the longest x2 1.59 us: fetch_rows(): outgoing = jnp.take(source, picked.reshape(-1), axis=0)]
    select_n x5 -> x0, other arithmetic: 2.09 us -> none  [the longest x2 1.05 us: fetch_rows(): outgoing = jnp.take(source, picked.reshape(-1), axis=0)]
    ppermute x1 -> x0, starting transfers between devices: 2.06 us -> none  [per_device(): later = lax.ppermute(rows, 'tm', [(w, w - 1) for w in range(1, windows)])]
  transfers between devices with their start and end apart: 2 -> 0, of which waited for: 1 -> 0; matrix products, arithmetic and copies ran while one was open for 1% -> 0% of each run, Pallas kernels for 0% -> 0%
where the time goes in v3:
time: 56.6 us; the launch traced here: 56.3 us
  Pallas kernels  53.7 us (95%)
  local copies, waits for them, and re-layouts  2.54 us (4%)
    pallas_call x1, Pallas kernels, exchange(): pl.pallas_call(functools.partial(exchange_kernel, plane, cores, slots), o...  41.2 us
    pallas_call x1, Pallas kernels, correlate(): pl.pallas_call(functools.partial(correlate_kernel, taps), out_shape=jax.S...  12.5 us
    unnamed x10, local copies, waits for them, and re-layouts  2.54 us

profile of v3, /device:TPU:1, one launch (start us, length us, event | category | flops | bytes accessed | tf_op | source)
XLA Modules:
  0.0 56.3 jit_solution(10722379629125215856)
XLA Ops:
  0.0 0.0 copy-start
  0.0 1.0 %copy-done = bf16[96,3,768]{2,0,1:T(8,128)(2,1)S(1)} copy-done((bf16[96,3,768]{2,0,1:T(8,128)(2,1)S(1)}, bf16[96,3,768]{2,0,1:T(8,128)(2,1)}, u32[]{:S(2)}) %copy-start) | copy-done | bytes 442392
  1.0 0.0 copy-start.1
  1.0 0.8 %copy-done.1 = bf16[1,1,48,600]{3,2,1,0:T(8,128)(2,1)S(1)} copy-done((bf16[1,1,48,600]{3,2,1,0:T(8,128)(2,1)S(1)}, bf16[1,1,48,600]{3,2,1,0:T(8,128)(2,1)}, u32[]{:S(2)}) %copy-start.1) | copy-done | bytes 57624
  1.8 0.0 copy-start.2
  1.8 0.7 %copy-done.2 = s32[32,16]{0,1:T(8,128)S(1)} copy-done((s32[32,16]{0,1:T(8,128)S(1)}, s32[32,16]{0,1:T(8,128)}, u32[]{:S(2)}) %copy-start.2) | copy-done | bytes 2072
  2.5 0.0 copy-start.3
  2.5 0.0 copy-start.4
  2.5 41.2 %shard_map.55 = (bf16[2,48,768]{2,1,0:T(8,128)(2,1)S(1)}, bf16[2,48,768]{2,1,0:T(8,128)(2,1)S(1)}, bf16[16,48,640]{2,1,0:T(8,128)(2,1)S(1)}) custom-call(s32[16,32]{1,0:T(8,128)S(1)} %bitcast.6, bf16[3,96,768]{2,1,0:T(8,128)(2,1)S(1)} %bitcast.4, bf16[48,600]{1,0:T(8,128)(2,1)S(1)} %bitcast.5), custom_call_target="tpu_custom_call" | custom-call | tf_op jit(solution)/shard_map/pallas_call | solution.py:447
  43.8 0.0 copy-done.3
  43.8 0.0 copy-done.4
  43.8 12.5 %shard_map.56 = f32[16,768]{1,0:T(8,128)} custom-call(s32[1,16,16]{2,1,0:T(8,128)S(1)} %copy-done.3, s32[1,16,16]{2,1,0:T(8,128)S(1)} %copy-done.4, bf16[2,48,768]{2,1,0:T(8,128)(2,1)S(1)} %get-tuple-element.8.near_ref, bf16[2,48,768]{2,1,0:T(8,128)(2,1)S(1)} %get-tuple-element.9.far_ref, bf16[16,48,640]{2,1,0:T(8,128)(2,1)S(1)} %get-tuple-element.10.tpl_ref), custom_call_target="tpu_custom_call" | custom-call | tf_op jit(solution)/shard_map/pallas_call | solution.py:162
Async XLA Ops:
  0.0 1.0 %copy-start = (bf16[96,3,768]{2,0,1:T(8,128)(2,1)S(1)}, bf16[96,3,768]{2,0,1:T(8,128)(2,1)}, u32[]{:S(2)}) copy-start(bf16[96,3,768]{2,0,1:T(8,128)(2,1)} %param.5) | copy-start | bytes 1327108
  1.0 0.8 %copy-start.1 = (bf16[1,1,48,600]{3,2,1,0:T(8,128)(2,1)S(1)}, bf16[1,1,48,600]{3,2,1,0:T(8,128)(2,1)}, u32[]{:S(2)}) copy-start(bf16[1,1,48,600]{3,2,1,0:T(8,128)(2,1)} %param.6) | copy-start | bytes 172804
  1.8 0.7 %copy-start.2 = (s32[32,16]{0,1:T(8,128)S(1)}, s32[32,16]{0,1:T(8,128)}, u32[]{:S(2)}) copy-start(s32[32,16]{0,1:T(8,128)} %param.7) | copy-start | bytes 6148
  2.5 41.3 %copy-start.3 = (s32[1,16,16]{2,1,0:T(8,128)S(1)}, s32[1,16,16]{2,1,0:T(8,128)}, u32[]{:S(2)}) copy-start(s32[1,16,16]{2,1,0:T(8,128)} %lists.1) | copy-start | bytes 3076
  2.5 41.3 %copy-start.4 = (s32[1,16,16]{2,1,0:T(8,128)S(1)}, s32[1,16,16]{2,1,0:T(8,128)}, u32[]{:S(2)}) copy-start(s32[1,16,16]{2,1,0:T(8,128)} %shifts.1) | copy-start | bytes 3076

commit v4 on v3

v4 whole, which is shorter than its diff:
```python
import functools

import jax
import jax.numpy as jnp
from jax import lax
from jax.experimental import pallas as pl
from jax.experimental.pallas import tpu as pltpu
from jax.sharding import PartitionSpec as P

STRIDE = 8
LANES = 128

MESH = pl.DeviceIdType.MESH
REACH = 2
EARLY = (2,)
ORDER = (1, 4, 3, 6, 5, 7)
FORWARD = 6


def iota(shape, dim):
    return lax.broadcasted_iota(jnp.int32, shape, dim)


def matched_filter_kernel(
    plane, cores, slots, taps, table_hbm, lists_hbm, shifts_hbm, wave_hbm, tpl_hbm, out_ref,
    table, lists, shifts, wave, raw, picked, chosen, outgoing, arrived, cross, near_ref, far_ref, all_ref,
    use_pair, rowidx, delays, picks, band, plain, shifted, xa, xb, inv, xa16, xb16, zs, acc,
    load_sems, out_sems, in_sems, pair_sems, halo_sems, line_sends, line_recvs, side_sends, side_recvs
):
    tm, spot = lax.axis_index("tm"), lax.axis_index("tmpl")
    windows = lax.axis_size("tm")
    chips = windows // cores
    chip, core = tm // cores, tm % cores
    half, place = spot // plane, spot % plane
    partner = (1 - half) * plane + place
    sibling = chip * cores + (1 - core)
    channels, stored, samples = wave.shape
    stations, groups = table.shape
    unit = arrived.shape[1]

    loads = [
        pltpu.make_async_copy(src, dst, load_sems.at[n])
        for n, (src, dst) in enumerate([(table_hbm, table), (wave_hbm, wave), (tpl_hbm, raw), (lists_hbm, lists), (shifts_hbm, shifts)])
    ]
    for load in loads:
        load.start()

    barrier = pltpu.get_barrier_semaphore()

    def greet(window, group):
        pl.semaphore_signal(barrier, inc=1, device_id=(window, group), device_id_type=MESH)

    def room(way):
        return chips - 1 - chip if way == 1 else chip

    def greet_plane(step, carry):
        greet(tm, half * plane + (place + step) % plane)
        return carry

    greet(tm, partner)
    lax.fori_loop(1, plane, greet_plane, 0)
    for step in range(1, REACH + 1):
        for way in (1, -1):
            @pl.when(room(way) >= step)
            def _(way=way, step=step):
                greet(tm + way * cores * step, spot)
    greet(sibling, spot)

    @pl.when((core == 0) & (chip > 0))
    def _():
        greet(tm - 1, spot)

    @pl.when((core == 1) & (chip < chips - 1))
    def _():
        greet(tm + 1, spot)

    loads[0].wait()
    base = spot * stored

    def scan(group, carry):
        count = 0
        found = [0] * slots
        for k in range(stations):
            gap = table[k, group] - base
            hit = (gap >= 0) & (gap < stored)
            found = [jnp.where(hit & (count == n), gap, found[n]) for n in range(slots)]
            count = count + jnp.where(hit, 1, 0)
        for n in range(slots):
            picked[group % plane, (group // plane) * slots + n] = found[n]
        return carry

    lax.fori_loop(0, groups, scan, 0)
    loads[1].wait()

    row = iota((unit, channels * stored), 0)
    column = iota((unit, channels * stored), 1)

    def choose(step, carry):
        want = jnp.where(row < 2 * slots * channels, row % channels * stored, -stored)
        for n in range(2 * slots):
            want = want + jnp.where(row // channels == n, picked[step, n], 0)
        chosen[pl.ds(pl.multiple_of(step * unit, unit), unit), :] = jnp.where(column == want, 1.0, 0.0).astype(chosen.dtype)
        return carry

    lax.fori_loop(0, plane, choose, 0)
    outgoing[...] = jnp.dot(
        chosen[...], wave[...].reshape(channels * stored, samples), preferred_element_type=jnp.float32
    ).astype(outgoing.dtype).reshape(outgoing.shape)
    arrived[place] = outgoing[place]

    spots = iota((stations * channels, plane * unit), 0)
    order = iota((stations * channels, plane * unit), 1)

    def collect(group, side):
        want = spots % channels
        owners = []
        for k in range(stations):
            station = table[k, group]
            owner = station // stored
            rank = 0
            for earlier in owners:
                rank = rank + jnp.where(earlier == owner, 1, 0)
            owners.append(owner)
            place_of = owner % plane * unit + (side * slots + rank) * channels
            place_of = jnp.where(owner // plane == half, place_of, -channels)
            want = want + jnp.where(spots // channels == k, place_of, 0)
        return jnp.where(order == want, 1.0, 0.0).astype(arrived.dtype)

    across = collect(partner, 1 - half)
    local = collect(spot, half)

    loads[2].wait()
    values = raw[...].astype(jnp.float32)
    centred = values - jnp.mean(values, axis=-1, keepdims=True)
    factor = lax.rsqrt(jnp.sum(centred * centred, axis=-1, keepdims=True) + 1e-06)
    all_ref[tm] = jnp.zeros(all_ref.shape[1:], all_ref.dtype)
    all_ref[tm, :, :taps] = (centred * factor).astype(all_ref.dtype)

    peers = plane + 1
    for step in range(1, REACH + 1):
        for way in (1, -1):
            peers = peers + (room(way) + chips - step) // chips
    peers = peers + (1 - core) * ((chip + chips - 1) // chips) + core * ((2 * chips - 2 - chip) // chips)
    pl.semaphore_wait(barrier, peers)

    def row_copy(step):
        to = (place + step) % plane
        return pltpu.make_async_remote_copy(
            src_ref=outgoing.at[to], dst_ref=arrived.at[place],
            send_sem=out_sems.at[step], recv_sem=in_sems.at[step],
            device_id=(tm, half * plane + to), device_id_type=MESH,
        )

    def line_copy(way, come, go):
        window = tm - way * cores * come
        lane = (1 - way) // 2
        return pltpu.make_async_remote_copy(
            src_ref=all_ref.at[window], dst_ref=all_ref.at[window],
            send_sem=line_sends.at[lane, come + go], recv_sem=line_recvs.at[lane, come + go],
            device_id=(tm + way * cores * go, spot), device_id_type=MESH,
        )

    def side_copy(way, come):
        window = tm - way * cores * come
        lane = (1 - way) // 2
        return pltpu.make_async_remote_copy(
            src_ref=all_ref.at[window], dst_ref=all_ref.at[window],
            send_sem=side_sends.at[lane, come], recv_sem=side_recvs.at[lane, come],
            device_id=(sibling, spot), device_id_type=MESH,
        )

    def send_rows(step, carry):
        row_copy(step).start()
        return carry

    def take_rows(step, carry):
        row_copy(step).wait_recv()
        return carry

    def sent_rows(step, carry):
        row_copy(step).wait_send()
        return carry

    lax.fori_loop(1, plane, send_rows, 0)
    for go in range(REACH, 0, -1):
        for way in (1, -1):
            @pl.when(room(way) >= go)
            def _(way=way, go=go):
                line_copy(way, 0, go).start()
    side_copy(1, 0).start()

    def receive(come):
        for way in (1, -1):
            @pl.when(room(-way) >= come)
            def _(way=way):
                line_copy(way, come, 0).wait_recv()
                if come % REACH == 0:
                    for go in range(min(REACH, chips - 1 - come), 0, -1):
                        @pl.when(room(way) >= go)
                        def _(go=go):
                            line_copy(way, come, go).start()
                side_copy(way, come).start()

    for come in EARLY:
        receive(come)

    tpls, nrc = lists.shape[0], stations * channels
    frames = samples // STRIDE
    padded = all_ref.shape[2]
    steps = taps // STRIDE + 1
    gap = iota((samples, LANES), 0) - STRIDE * iota((samples, LANES), 1)
    for e in range(STRIDE):
        picks[e] = jnp.where(gap == e, 1.0, 0.0).astype(picks.dtype)
    ahead = iota((2 * LANES, LANES), 0) - iota((2 * LANES, LANES), 1)
    band[...] = jnp.where((ahead >= 0) & (ahead < taps // STRIDE), 1.0, 0.0).astype(band.dtype)
    for slot in range(2):
        for c in range(channels):
            zs[slot, c, STRIDE * steps :, :] = jnp.zeros((padded - STRIDE * steps, LANES), zs.dtype)
    acc[...] = jnp.zeros_like(acc)

    loads[3].wait()
    loads[4].wait()
    who, lag = lists[...], shifts[...]
    entry = iota(who.shape, 1)
    first, late = jnp.zeros_like(who), jnp.zeros_like(who)
    for r in range(stations):
        hit = who == r
        first = jnp.where(entry == r, jnp.max(jnp.where(hit, entry, 0), axis=1, keepdims=True), first)
        late = jnp.where(entry == r, jnp.max(jnp.where(hit, lag, 0), axis=1, keepdims=True), late)
    use_pair[0] = first * channels + iota(who.shape, 0) * nrc
    use_pair[1] = late
    uses = [
        pltpu.make_async_copy(use_pair.at[n], dst, load_sems.at[5 + n]) for n, dst in enumerate((rowidx, delays))
    ]
    for use in uses:
        use.start()

    lax.fori_loop(1, plane, take_rows, 0)

    def pull(hot):
        rows = arrived[...].reshape(plane * unit, samples)
        return jnp.dot(hot, rows, preferred_element_type=jnp.float32).astype(arrived.dtype)

    cross[...] = pull(across)
    pair = pltpu.make_async_remote_copy(
        src_ref=cross, dst_ref=far_ref.at[0], send_sem=pair_sems.at[0], recv_sem=pair_sems.at[1],
        device_id=(tm, partner), device_id_type=MESH,
    )
    pair.start()
    near_ref[0] = pull(local)

    def halo(n):
        ref = (near_ref, far_ref)[n]
        return pltpu.make_async_remote_copy(
            src_ref=ref.at[0], dst_ref=ref.at[1], send_sem=halo_sems.at[n, 0], recv_sem=halo_sems.at[n, 1],
            device_id=((tm + windows - 1) % windows, spot), device_id_type=MESH,
        )

    @pl.when(tm > 0)
    def _():
        halo(0).start()

    @pl.when(tm == windows - 1)
    def _():
        near_ref[1] = jnp.zeros(near_ref.shape[1:], near_ref.dtype)
        far_ref[1] = jnp.zeros(far_ref.shape[1:], far_ref.dtype)

    lane = iota((STRIDE, LANES), 1)
    sub = iota((STRIDE, LANES), 0)

    def spread_taps(window):
        plain[...] = all_ref[window].astype(jnp.float32)

        def eight(part, carry):
            start = pl.multiple_of(part * STRIDE, STRIDE)
            for n in range(STRIDE):
                row = plain[pl.ds(start + n, 1), :]
                before = jnp.zeros((STRIDE, LANES), jnp.float32)
                for b in range(padded // LANES):
                    here = pltpu.roll(
                        jnp.broadcast_to(row[:, LANES * b : LANES * (b + 1)], (STRIDE, LANES)),
                        0, axis=1, stride=1, stride_axis=0,
                    )
                    shifted[window * nrc + start + n, :, LANES * b : LANES * (b + 1)] = jnp.where(
                        lane < sub, before, here
                    ).astype(shifted.dtype)
                    before = here
            return carry

        lax.fori_loop(0, nrc // STRIDE, eight, 0)

    def take_line(come):
        for way in (1, -1):
            @pl.when(room(-way) >= come)
            def _(way=way):
                spread_taps(tm - way * cores * come)

    def take_side(come):
        for way in (1, -1):
            @pl.when(room(-way) >= come)
            def _(way=way):
                side_copy(way, come).wait()
                spread_taps(sibling - way * cores * come)

    spread_taps(tm)
    take_line(REACH)
    side_copy(1, 0).wait()
    spread_taps(sibling)
    last = REACH
    for come in ORDER:
        receive(come)
        if come == FORWARD:
            pair.wait_recv()

            @pl.when(tm > 0)
            def _():
                halo(1).start()

        take_line(come)
        take_side(last)
        last = come
    own = near_ref[0].astype(jnp.float32) + far_ref[0].astype(jnp.float32)
    own = own.astype(jnp.bfloat16)
    for e in range(STRIDE):
        xa[:, e, :] = jnp.dot(own, picks[e], preferred_element_type=jnp.float32)
    take_side(last)

    for come in range(0, chips, REACH):
        for go in range(1, min(REACH, chips - 1 - come) + 1):
            for way in (1, -1):
                @pl.when((room(-way) >= come) & (room(way) >= go))
                def _(way=way, come=come, go=go):
                    line_copy(way, come, go).wait_send()
    lax.fori_loop(1, plane, sent_rows, 0)
    pair.wait_send()

    @pl.when(tm < windows - 1)
    def _():
        halo(0).wait_recv()
        halo(1).wait_recv()

    @pl.when(tm > 0)
    def _():
        halo(0).wait_send()
        halo(1).wait_send()

    for use in uses:
        use.wait()
    later_rows = near_ref[1].astype(jnp.float32) + far_ref[1].astype(jnp.float32)
    later_rows = later_rows.astype(jnp.bfloat16)
    flat_lane = iota((nrc, LANES), 1)
    for e in range(STRIDE):
        phase = jnp.dot(later_rows, picks[e], preferred_element_type=jnp.float32)
        later = pltpu.roll(phase, frames, axis=1)
        xa[:, e, :] = jnp.where(flat_lane < frames, xa[:, e, :], later)
        xb[:, e, :] = later

    flat = jnp.concatenate([xa[...].reshape(nrc * STRIDE, LANES), xb[...].reshape(nrc * STRIDE, LANES)], axis=1)
    square = flat * flat
    high = square.astype(jnp.bfloat16)
    low = (square - high.astype(jnp.float32)).astype(jnp.bfloat16)

    def banded(v):
        return jnp.dot(v, band[...], preferred_element_type=jnp.float32)

    def octet(v):
        v = v.reshape(nrc, STRIDE, LANES)
        row = iota((nrc, STRIDE, LANES), 1)
        for k in (1, 2, 4):
            nxt = pltpu.roll(v, LANES - 1, axis=2)
            v = v + pltpu.roll(jnp.where(row < k, nxt, v), STRIDE - k, axis=1)
        return v

    wsum = octet(banded(flat.astype(jnp.bfloat16)))
    wsq = octet(banded(high) + banded(low))
    inv[...] = lax.rsqrt(jnp.maximum(wsq - wsum * wsum / taps, 1.0))

    lane16 = iota((2 * STRIDE, LANES), 1)
    wide = iota((nrc, STRIDE, LANES), 2)
    next_b = pltpu.roll(xb[...], LANES - 1, axis=2)
    next_a = jnp.where(wide < LANES - 1, pltpu.roll(xa[...], LANES - 1, axis=2), next_b)
    xa16[...] = jnp.concatenate([xa[...], next_a], axis=1).astype(jnp.bfloat16)
    xb16[...] = jnp.concatenate([xb[...], next_b], axis=1).astype(jnp.bfloat16)
    def build(r, slot):
        for c in range(channels):
            rc = r * channels + c
            a, b = xa16[rc], xb16[rc]
            for i in range(0, steps, 2):
                mixed = jnp.where(lane16 < i, b, a) if i else a
                zs[slot, c, STRIDE * i : STRIDE * (i + 2), :] = pltpu.roll(mixed, LANES - i, axis=1) if i else a

    def multiply(r, slot):
        products = []
        for c in range(channels):
            left = jnp.concatenate([shifted[rowidx[t, r] + c] for t in range(tpls)], axis=0)
            products.append(jnp.dot(left, zs[slot, c], preferred_element_type=jnp.float32))
        return products

    def settle(r, products):
        ratio = sum(
            products[c].reshape(tpls, STRIDE, LANES) * inv[r * channels + c][None] for c in range(channels)
        )
        for t in range(tpls):
            m = delays[t, r]
            f = m // STRIDE
            e = m - f * STRIDE
            near = pltpu.roll(ratio[t], (LANES - f) % LANES, axis=1)
            far = pltpu.roll(near, LANES - 1, axis=1)
            acc[t] += pltpu.roll(jnp.where(sub < e, far, near), (STRIDE - e) % STRIDE, axis=0)

    build(0, 0)

    def pair_of(p, carry):
        first = 2 * p
        products = multiply(first, 0)
        build(first + 1, 1)
        settle(first, products)
        products = multiply(first + 1, 1)
        build(jnp.minimum(first + 2, stations - 1), 0)
        settle(first + 1, products)
        return carry

    lax.fori_loop(0, stations // 2, pair_of, 0)

    total = acc[...].reshape(tpls * STRIDE, LANES)
    p1 = total.astype(jnp.bfloat16)
    rest = total - p1.astype(jnp.float32)
    p2 = rest.astype(jnp.bfloat16)
    p3 = (rest - p2.astype(jnp.float32)).astype(jnp.bfloat16)
    spots = iota((LANES, samples), 1) // STRIDE
    spread_out = jnp.where(spots == iota((LANES, samples), 0), 1.0, 0.0).astype(jnp.bfloat16)

    def placed(v):
        return jnp.dot(v, spread_out, preferred_element_type=jnp.float32)

    wide = (placed(p1) + placed(p2) + placed(p3)).reshape(tpls, STRIDE, samples)
    mine = iota((tpls, STRIDE, samples), 2) % STRIDE == iota((tpls, STRIDE, samples), 1)
    out_ref[...] = jnp.sum(jnp.where(mine, wide, 0.0), axis=1)


def matched_filter(table, lists, shifts, wave, tpl, slots, padded):
    windows = lax.axis_size("tm")
    cores = 2
    stations, groups = table.shape
    plane = groups // 2
    channels, stored, samples = wave.shape
    unit = -(-2 * slots * channels // 8) * 8
    nrc = stations * channels
    tpls = lists.shape[0]
    chips = windows // cores
    operands = (table, lists, shifts, wave, tpl)
    return pl.pallas_call(
        functools.partial(matched_filter_kernel, plane, cores, slots, tpl.shape[1]),
        out_shape=jax.ShapeDtypeStruct((tpls, samples), jnp.float32),
        in_specs=[pl.BlockSpec(memory_space=pltpu.HBM)] * len(operands),
        out_specs=pl.BlockSpec(memory_space=pltpu.VMEM),
        scratch_shapes=[
            pltpu.SMEM(table.shape, jnp.int32),
            pltpu.VMEM(lists.shape, jnp.int32),
            pltpu.VMEM(shifts.shape, jnp.int32),
            pltpu.VMEM(wave.shape, wave.dtype),
            pltpu.VMEM(tpl.shape, tpl.dtype),
            pltpu.SMEM((plane, 2 * slots), jnp.int32),
            pltpu.VMEM((plane * unit, channels * stored), jnp.bfloat16),
            pltpu.VMEM((plane, unit, samples), jnp.bfloat16),
            pltpu.VMEM((plane, unit, samples), jnp.bfloat16),
            pltpu.VMEM((nrc, samples), jnp.bfloat16),
            pltpu.VMEM((2, nrc, samples), jnp.bfloat16),
            pltpu.VMEM((2, nrc, samples), jnp.bfloat16),
            pltpu.VMEM((windows, tpl.shape[0], padded), jnp.bfloat16),
            pltpu.VMEM((2, *lists.shape), jnp.int32),
            pltpu.SMEM(lists.shape, jnp.int32),
            pltpu.SMEM(lists.shape, jnp.int32),
            pltpu.VMEM((STRIDE, samples, LANES), jnp.bfloat16),
            pltpu.VMEM((2 * LANES, LANES), jnp.bfloat16),
            pltpu.VMEM((nrc, padded), jnp.float32),
            pltpu.VMEM((tpls * nrc, STRIDE, padded), jnp.bfloat16),
            pltpu.VMEM((nrc, STRIDE, LANES), jnp.float32),
            pltpu.VMEM((nrc, STRIDE, LANES), jnp.float32),
            pltpu.VMEM((nrc, STRIDE, LANES), jnp.float32),
            pltpu.VMEM((nrc, 2 * STRIDE, LANES), jnp.bfloat16),
            pltpu.VMEM((nrc, 2 * STRIDE, LANES), jnp.bfloat16),
            pltpu.VMEM((2, channels, padded, LANES), jnp.bfloat16),
            pltpu.VMEM((tpls, STRIDE, LANES), jnp.float32),
            pltpu.SemaphoreType.DMA((7,)),
            pltpu.SemaphoreType.DMA((plane,)),
            pltpu.SemaphoreType.DMA((plane,)),
            pltpu.SemaphoreType.DMA((2,)),
            pltpu.SemaphoreType.DMA((2, 2)),
            pltpu.SemaphoreType.DMA((2, chips)),
            pltpu.SemaphoreType.DMA((2, chips)),
            pltpu.SemaphoreType.DMA((2, chips)),
            pltpu.SemaphoreType.DMA((2, chips)),
        ],
        compiler_params=pltpu.CompilerParams(
            collective_id=0, has_side_effects=True, vmem_limit_bytes=40 << 20
        ),
    )(*(pltpu.with_memory_space_constraint(v, pltpu.HBM) for v in operands))


def per_device(waveforms, templates, group_stations, template_rows, moveouts):
    slots = max(2, 2 * group_stations.shape[1] // lax.axis_size("tmpl"))
    padded = (templates.shape[3] + LANES - 1) // LANES * LANES
    return matched_filter(
        group_stations.T, template_rows[0], moveouts[0], waveforms.transpose(1, 0, 2), templates[0, 0], slots, padded
    )[None]


def solution(mesh):
    in_specs = (
        P("tmpl", None, "tm"),
        P("tmpl", "tm", None, None),
        P(),
        P("tmpl", None, None),
        P("tmpl", None, None),
    )
    out_specs = P("tmpl", None, "tm")
    return jax.shard_map(
        per_device, mesh=mesh, in_specs=in_specs, out_specs=out_specs, check_vma=False
    )
```

time: 56.6 us -> 49.8 us (0.88)
  Pallas kernels: 53.7 us -> 49 us
  local copies, waits for them, and re-layouts: 2.54 us -> 0.62 us
    pallas_call x2 -> x1, Pallas kernels: 53.7 us -> 49 us  [matched_filter(): pl.pallas_call(functools.partial(matched_filter_kernel, plane, cores, slo...]
    unnamed x10 -> x1, local copies, waits for them, and re-layouts: 2.54 us -> 0.62 us
where the time goes in v4:
time: 49.8 us; the launch traced here: 49.7 us
  Pallas kernels  49 us (98%)
  local copies, waits for them, and re-layouts  0.62 us (1%)
    pallas_call x1, Pallas kernels, matched_filter(): pl.pallas_call(functools.partial(matched_filter_kernel, plane, cores, slo...  49 us

profile of v4, /device:TPU:1, one launch (start us, length us, event | category | flops | bytes accessed | tf_op | source)
XLA Modules:
  0.0 49.7 jit_solution(10976024853070586778)
XLA Ops:
  0.0 49.0 %shard_map.55 = f32[16,768]{1,0:T(8,128)S(1)} custom-call(s32[16,32]{1,0:T(8,128)} %bitcast.9, s32[16,16]{1,0:T(8,128)} %bitcast.10, s32[16,16]{1,0:T(8,128)} %bitcast.11, bf16[3,96,768]{2,1,0:T(8,128)(2,1)} %bitcast.7, bf16[48,600]{1,0:T(8,128)(2,1)} %bitcast.8), custom_call_target="tpu_custom_call" | custom-call | tf_op jit(solution)/shard_map/pallas_call | solution.py:452
  49.0 0.6 %copy.7 = f32[1,16,768]{2,1,0:T(8,128)} copy(f32[1,16,768]{2,1,0:T(8,128)S(1)} %bitcast.6) | data formatting | bytes 98304

commit v5 on v4

--- a/solution.py
+++ b/solution.py
@@ -11,10 +11,11 @@
 LANES = 128
 
 MESH = pl.DeviceIdType.MESH
-REACH = 2
+HOPS = {0: 2, 2: 3, 5: 2}
+REACH = max(HOPS.values())
 EARLY = (2,)
-ORDER = (1, 4, 3, 6, 5, 7)
-FORWARD = 6
+ORDER = (1, 5, 4, 3, 6, 7)
+FORWARD = 3
 
 
 def iota(shape, dim):
@@ -42,9 +43,6 @@
         pltpu.make_async_copy(src, dst, load_sems.at[n])
         for n, (src, dst) in enumerate([(table_hbm, table), (wave_hbm, wave), (tpl_hbm, raw), (lists_hbm, lists), (shifts_hbm, shifts)])
     ]
-    for load in loads:
-        load.start()
-
     barrier = pltpu.get_barrier_semaphore()
 
     def greet(window, group):
@@ -53,12 +51,17 @@
     def room(way):
         return chips - 1 - chip if way == 1 else chip
 
+    def start_loads():
+        for load in loads:
+            load.start()
+
     def greet_plane(step, carry):
         greet(tm, half * plane + (place + step) % plane)
         return carry
 
     greet(tm, partner)
     lax.fori_loop(1, plane, greet_plane, 0)
+    start_loads()
     for step in range(1, REACH + 1):
         for way in (1, -1):
             @pl.when(room(way) >= step)
@@ -181,12 +184,16 @@
         row_copy(step).wait_send()
         return carry
 
-    lax.fori_loop(1, plane, send_rows, 0)
-    for go in range(REACH, 0, -1):
+    def send_line(go):
         for way in (1, -1):
             @pl.when(room(way) >= go)
-            def _(way=way, go=go):
+            def _(way=way):
                 line_copy(way, 0, go).start()
+
+    send_line(HOPS[0])
+    lax.fori_loop(1, plane, send_rows, 0)
+    for go in range(HOPS[0] - 1, 0, -1):
+        send_line(go)
     side_copy(1, 0).start()
 
     def receive(come):
@@ -194,8 +201,8 @@
             @pl.when(room(-way) >= come)
             def _(way=way):
                 line_copy(way, come, 0).wait_recv()
-                if come % REACH == 0:
-                    for go in range(min(REACH, chips - 1 - come), 0, -1):
+                if come in HOPS:
+                    for go in range(HOPS[come], 0, -1):
                         @pl.when(room(way) >= go)
                         def _(go=go):
                             line_copy(way, come, go).start()
@@ -303,10 +310,10 @@
                 spread_taps(sibling - way * cores * come)
 
     spread_taps(tm)
-    take_line(REACH)
+    take_line(EARLY[0])
     side_copy(1, 0).wait()
     spread_taps(sibling)
-    last = REACH
+    last = EARLY[0]
     for come in ORDER:
         receive(come)
         if come == FORWARD:
@@ -325,8 +332,8 @@
         xa[:, e, :] = jnp.dot(own, picks[e], preferred_element_type=jnp.float32)
     take_side(last)
 
-    for come in range(0, chips, REACH):
-        for go in range(1, min(REACH, chips - 1 - come) + 1):
+    for come in HOPS:
+        for go in range(1, HOPS[come] + 1):
             for way in (1, -1):
                 @pl.when((room(-way) >= come) & (room(way) >= go))
                 def _(way=way, come=come, go=go):

time: 49.8 us -> 49.5 us (level)
  the two profiles are of different devices: /device:TPU:1 before, /device:TPU:97 now
where the time goes in v5:
time: 49.5 us; the launch traced here: 49.3 us
  Pallas kernels  48.7 us (98%)
  local copies, waits for them, and re-layouts  0.62 us (1%)
    pallas_call x1, Pallas kernels, matched_filter(): pl.pallas_call(functools.partial(matched_filter_kernel, plane, cores, slo...  48.7 us

profile of v5, /device:TPU:97, one launch (start us, length us, event | category | flops | bytes accessed | tf_op | source)
XLA Modules:
  0.0 49.3 jit_solution(3354134666207341126)
XLA Ops:
  0.0 48.7 %shard_map.55 = f32[16,768]{1,0:T(8,128)S(1)} custom-call(s32[16,32]{1,0:T(8,128)} %bitcast.9, s32[16,16]{1,0:T(8,128)} %bitcast.10, s32[16,16]{1,0:T(8,128)} %bitcast.11, bf16[3,96,768]{2,1,0:T(8,128)(2,1)} %bitcast.7, bf16[48,600]{1,0:T(8,128)(2,1)} %bitcast.8), custom_call_target="tpu_custom_call" | custom-call | tf_op jit(solution)/shard_map/pallas_call | solution.py:459
  48.7 0.6 %copy.7 = f32[1,16,768]{2,1,0:T(8,128)} copy(f32[1,16,768]{2,1,0:T(8,128)S(1)} %bitcast.6) | data formatting | bytes 98304
